TPU v7x, 32 devices: a whole 2x2x4 slice. The times are simulated.
32 devices in a mesh: grp: 4 (over x, core), gx: 2 (over y), gy: 4 (over z).
Axes of the slice: x: 2, y: 2, z: 4, core: 2. Of those that a mesh axis runs over, the one named last changes fastest.
Arguments:
- sources: float32 [4, 8, 32, 512], P('grp', 'gx', 'gy'), may hold values from -4.5 to 5.5
- diagonal: float32 [8, 32, 512], P('gx', 'gy'), may hold values from 0.02 to 0.3
- coarse_ids: int32 [8, 32, 512], P('gx', 'gy'), may hold values from 0 to 255, as said below
- coarse_inverse: float32 [256, 256], replicated, may hold values from -1 to 3
- omega_rows: float32 [4, 32], replicated, may hold values from -5 to 5
- psi: float32 [32, 8, 32, 512], P(None, 'gx', 'gy', 'grp'), may hold values from -0.015625 to 0.015625
- phi: float32 [64, 8, 32, 512], P(None, 'gx', 'gy', 'grp'), may hold values from -0.015625 to 0.015625
- xi_cols: float32 [64, 4], replicated, may hold values from -5 to 5
- range_sketch: float32 [32, 8, 32, 512], P(None, 'gx', 'gy', 'grp'), may hold values from -3 to 3
- core_sketch: float32 [64, 64], replicated, may hold values from -2 to 2
Outputs:
- range_new: float32 [32, 8, 32, 512], P(None, 'gx', 'gy', 'grp')
- corange_cols: float32 [32, 4], replicated
- core_new: float32 [64, 64], replicated
Inputs may be any that keep to these rules, and one draw needn't show every extreme that they name: `coarse_ids`: the grid is cut into 4, 4 and 16 non-empty ranges of consecutive cells along the three dimensions; coarse cell (a * 4 + b) * 16 + c is the box of ranges a, b, c.
All inputs are finite; a program needn't handle non-finite values.
Results may differ from a plain program's by a relative error of at most 0.0003.
Values sent between devices are 32-bit elements; how exact they have to be, the bound alone decides.
No kernel may reach another device: no remote copies, remote signals or barrier semaphores. Data moves between devices by JAX's collectives and lax.ppermute only.
A program may use at most 64 MiB of HBM per device.

v0:
```python
import jax
import jax.numpy as jnp
from jax import lax
from jax.sharding import PartitionSpec as P

OUTER = 2
SWEEPS = 4
XY_CUTS = 4
Z_CUTS = 16


jacobi_weight = 2.0 / 3.0
highest = lax.Precision.HIGHEST


def with_halo(cells, sides, width):
    for axis, dim in sides:
        count = lax.axis_size(axis)
        ends = count - 1
        head = lax.slice_in_dim(cells, 0, width, axis=dim)
        tail = lax.slice_in_dim(cells, cells.shape[dim] - width, cells.shape[dim], axis=dim)
        cells = jnp.concatenate(
            [
                lax.ppermute(tail, axis, [(i, (i + 1) % count) for i in range(ends)]),
                cells,
                lax.ppermute(head, axis, [((i + 1) % count, i) for i in range(ends)]),
            ],
            axis=dim,
        )
    return cells


def neighbour_image(widened, diagonal):
    center = widened[1:-1, 1:-1]
    beside = widened[2:, 1:-1] + widened[:-2, 1:-1]
    beside = beside + widened[1:-1, 2:] + widened[1:-1, :-2]
    padded = jnp.pad(center, ((0, 0), (0, 0), (1, 1)))
    beside = beside + padded[:, :, 2:] + padded[:, :, :-2]
    return (center, (6.0 + diagonal) * center - beside)


def smooth_once(widened, source, diagonal):
    center, applied = neighbour_image(widened, diagonal)
    return center + jacobi_weight * (source - applied) / (6.0 + diagonal)


def widen_faces(values):
    return with_halo(values, (("gx", 0), ("gy", 1)), 1)


def axis_maps(coarse_ids):
    ranks_x = coarse_ids[:, 0, 0] // (XY_CUTS * Z_CUTS)
    ranks_y = coarse_ids[0, :, 0] // Z_CUTS % XY_CUTS
    ranks_z = coarse_ids[0, 0, :] % Z_CUTS
    cuts_xy = jnp.arange(XY_CUTS, dtype=jnp.int32)
    cuts_z = jnp.arange(Z_CUTS, dtype=jnp.int32)
    map_x = (ranks_x[:, None] == cuts_xy[None, :]).astype(jnp.float32)
    map_y = (ranks_y[:, None] == cuts_xy[None, :]).astype(jnp.float32)
    map_z = (ranks_z[:, None] == cuts_z[None, :]).astype(jnp.float32)
    return (map_x, map_y, map_z)


def restrict(values, maps):
    map_x, map_y, map_z = maps
    rows_x, rows_y, cells_z = values.shape
    along_z = jnp.dot(values.reshape(rows_x * rows_y, cells_z), map_z, precision=highest)
    along_z = along_z.reshape(rows_x, rows_y, Z_CUTS)
    along_y = jnp.einsum("xyc,yb->xbc", along_z, map_y, precision=highest)
    along_x = jnp.einsum("xbc,xa->abc", along_y, map_x, precision=highest)
    return along_x.reshape(-1)


def prolong(correction, maps, extent):
    map_x, map_y, map_z = maps
    boxes = correction.reshape(XY_CUTS, XY_CUTS, Z_CUTS)
    over_x = jnp.einsum("abc,xa->xbc", boxes, map_x, precision=highest)
    over_y = jnp.einsum("xbc,yb->xyc", over_x, map_y, precision=highest)
    spread = jnp.dot(over_y.reshape(extent[0] * extent[1], Z_CUTS), map_z.T, precision=highest)
    return spread.reshape(extent)


def body(
    sources,
    diagonal,
    coarse_ids,
    coarse_inverse,
    omega_rows,
    psi,
    phi,
    xi_cols,
    range_sketch,
    core_sketch,
):
    source = sources[0]
    rows_x, rows_y, cells_z = source.shape
    coarse = coarse_inverse.shape[0]
    total_cells = rows_x * lax.axis_size("gx") * rows_y * lax.axis_size("gy") * cells_z
    scale_factor = coarse / total_cells
    maps = axis_maps(coarse_ids)
    stacked = jnp.stack([source, diagonal])
    margin = with_halo(stacked, (("gx", 1), ("gy", 2)), 2)
    place_x = lax.axis_index("gx") * rows_x + jnp.arange(rows_x + 4) - 2
    place_y = lax.axis_index("gy") * rows_y + jnp.arange(rows_y + 4) - 2
    inside_x = ((place_x >= 0) & (place_x < rows_x * lax.axis_size("gx"))).astype(jnp.float32)
    inside_y = ((place_y >= 0) & (place_y < rows_y * lax.axis_size("gy"))).astype(jnp.float32)
    inside = inside_x[:, None, None] * inside_y[None, :, None]
    pressure = jnp.zeros_like(source)
    for outer_step in range(OUTER):
        if outer_step == 0:
            residual = source
        else:
            residual = source - neighbour_image(widen_faces(pressure), diagonal)[1]
        coarse_rhs = lax.psum(restrict(residual, maps), ("gx", "gy"))
        correction = jnp.dot(coarse_inverse, coarse_rhs * scale_factor, precision=highest)
        pressure = pressure + prolong(correction, maps, source.shape)
        for sweep_step in range(SWEEPS // 2):
            widened = with_halo(pressure, (("gx", 0), ("gy", 1)), 2)
            halfway = (
                smooth_once(widened, margin[0, 1:-1, 1:-1], margin[1, 1:-1, 1:-1])
                * inside[1:-1, 1:-1]
            )
            pressure = smooth_once(halfway, source, diagonal)
    snapshot = lax.all_to_all(pressure[None], "grp", split_axis=3, concat_axis=0, tiled=True)
    columns = snapshot.reshape(snapshot.shape[0], -1)
    range_flat = range_sketch.reshape(range_sketch.shape[0], -1)
    range_new = range_flat + jnp.einsum("tk,tc->kc", omega_rows, columns, precision=highest)
    corange_part = jnp.einsum(
        "lc,tc->lt", psi.reshape(psi.shape[0], -1), columns, precision=highest
    )
    core_part = jnp.einsum("sc,tc->st", phi.reshape(phi.shape[0], -1), columns, precision=highest)
    corange_cols, core_images = lax.psum((corange_part, core_part), ("grp", "gx", "gy"))
    core_new = core_sketch + jnp.dot(core_images, xi_cols.T, precision=highest)
    return (range_new.reshape(range_sketch.shape), corange_cols, core_new)


def solution(mesh):
    return jax.shard_map(
        body,
        mesh=mesh,
        in_specs=(
            P("grp", "gx", "gy", None),
            P("gx", "gy", None),
            P("gx", "gy", None),
            P(),
            P(),
            P(None, "gx", "gy", "grp"),
            P(None, "gx", "gy", "grp"),
            P(),
            P(None, "gx", "gy", "grp"),
            P(),
        ),
        out_specs=(P(None, "gx", "gy", "grp"), P(), P()),
        check_vma=False,
    )
```

profile of v0, /device:TPU:0, one launch (start us, length us, event | category | flops | bytes accessed | tf_op | source)
XLA Modules:
  0.0 196.1 jit_solution(4064539406611665309)
XLA Ops:
  0.6 0.8 slice.305
  1.4 0.8 slice_reduce_fusion
  2.2 0.9 slice_reduce_fusion.1
  3.1 1.0 convolution_bitcast_fusion.5
  4.3 0.3 fusion.116
  4.7 23.3 %psum.28 = f32[256]{0:T(256)S(1)} all-reduce(f32[256]{0:T(256)S(1)} %reshape.211), channel_id=1, replica_groups=mesh['grp'=4,'gx'=2,'gy'=4] {'gx','gy'}, use_global_device_ids=true, to_apply=%region_0.1 | all-reduce | flops 256 | bytes 2048 | tf_op jit(solution)/shard_map/psum | solution.py:113
  28.0 0.3 fusion.138
  29.0 2.5 %collective-permute-start = (f32[2,8,512]{2,1,0:T(8,128)S(1)}, f32[2,8,512]{2,1,0:T(8,128)S(1)}, u32[]{:S(2)}, u32[]{:S(2)}) collective-permute-start(f32[2,8,512]{2,1,0:T(8,128)S(1)} %get-tuple-element.30), channel_id=1, source_target_pairs={{0,4},{1,5},{2,6},{3,7},{8,12},{9,13},{10,14},{11,15},{16,20},{17,... | collective-permute-start | bytes 98312 | tf_op jit(solution)/shard_map/ppermute | solution.py:24
  31.5 1.3 collective-permute-start.1
  32.9 4.5 %collective-permute-start.4 = (f32[2,2,8,512]{3,2,1,0:T(8,128)S(1)}, f32[2,2,8,512]{3,2,1,0:T(8,128)S(1)}, u32[]{:S(2)}, u32[]{:S(2)}) collective-permute-start(f32[2,2,8,512]{3,2,1,0:T(8,128)S(1)} %get-tuple-element.16), channel_id=1, source_target_pairs={{0,4},{1,5},{2,6},{3,7},{8,12},{9,13},{10,14},{11,15},{16,20},{17,... | collective-permute-start | bytes 196616 | tf_op jit(solution)/shard_map/ppermute | solution.py:24
  37.4 1.3 collective-permute-start.5
  38.9 1.3 collective-permute-start.2
  40.2 1.3 collective-permute-start.3
  41.5 2.0 %collective-permute-done.5 = f32[2,2,8,512]{3,2,1,0:T(8,128)S(1)} collective-permute-done((f32[2,2,8,512]{3,2,1,0:T(8,128)S(1)}, f32[2,2,8,512]{3,2,1,0:T(8,128)S(1)}, u32[]{:S(2)}, u32[]{:S(2)}) %collective-permute-start.5) | collective-permute-done | bytes 65568 | tf_op jit(solution)/shard_map/ppermute | solution.py:26
  43.6 2.5 %collective-permute-start.6 = (f32[2,8,2,512]{3,2,1,0:T(2,128)S(1)}, f32[2,8,2,512]{3,2,1,0:T(2,128)S(1)}, u32[]{:S(2)}, u32[]{:S(2)}) collective-permute-start(f32[2,8,2,512]{3,2,1,0:T(2,128)S(1)} %get-tuple-element.8), channel_id=1, source_target_pairs={{0,1},{1,2},{2,3},{4,5},{5,6},{6,7},{8,9},{9,10},{10,11},{12,13},{... | collective-permute-start | bytes 196616 | tf_op jit(solution)/shard_map/ppermute | solution.py:24
  46.2 1.3 collective-permute-start.7
  47.6 0.5 collective-permute-done.6
  48.0 4.3 %collective-permute-done.7 = f32[2,8,2,512]{3,2,1,0:T(2,128)S(1)} collective-permute-done((f32[2,8,2,512]{3,2,1,0:T(2,128)S(1)}, f32[2,8,2,512]{3,2,1,0:T(2,128)S(1)}, u32[]{:S(2)}, u32[]{:S(2)}) %collective-permute-start.7) | collective-permute-done | bytes 65568 | tf_op jit(solution)/shard_map/ppermute | solution.py:26
  52.7 4.5 %collective-permute-start.8 = (f32[2,8,512]{2,1,0:T(8,128)S(1)}, f32[2,8,512]{2,1,0:T(8,128)S(1)}, u32[]{:S(2)}, u32[]{:S(2)}) collective-permute-start(f32[2,8,512]{2,1,0:T(8,128)S(1)} %get-tuple-element.28), channel_id=1, source_target_pairs={{0,4},{1,5},{2,6},{3,7},{8,12},{9,13},{10,14},{11,15},{16,20},{17,... | collective-permute-start | bytes 98312 | tf_op jit(solution)/shard_map/ppermute | solution.py:24
  57.3 1.3 collective-permute-start.9
  58.6 0.3 collective-permute-done.8
  58.9 4.2 %collective-permute-done.9 = f32[2,8,512]{2,1,0:T(8,128)S(1)} collective-permute-done((f32[2,8,512]{2,1,0:T(8,128)S(1)}, f32[2,8,512]{2,1,0:T(8,128)S(1)}, u32[]{:S(2)}, u32[]{:S(2)}) %collective-permute-start.9) | collective-permute-done | bytes 32800 | tf_op jit(solution)/shard_map/ppermute | solution.py:26
  63.1 1.9 collective-permute-start.10
  65.0 1.3 collective-permute-start.11
  66.3 0.3 collective-permute-done.10
  66.6 4.2 %collective-permute-done.11 = f32[8,2,512]{2,1,0:T(2,128)S(1)} collective-permute-done((f32[8,2,512]{2,1,0:T(2,128)S(1)}, f32[8,2,512]{2,1,0:T(2,128)S(1)}, u32[]{:S(2)}, u32[]{:S(2)}) %collective-permute-start.11) | collective-permute-done | bytes 32800 | tf_op jit(solution)/shard_map/ppermute | solution.py:26
  71.3 1.3 collective-permute-start.12
  72.6 4.5 %collective-permute-start.13 = (f32[1,8,512]{2,1,0:T(8,128)S(1)}, f32[1,8,512]{2,1,0:T(8,128)S(1)}, u32[]{:S(2)}, u32[]{:S(2)}) collective-permute-start(f32[1,8,512]{2,1,0:T(8,128)S(1)} %get-tuple-element.26), channel_id=1, source_target_pairs={{0,4},{1,5},{2,6},{3,7},{8,12},{9,13},{10,14},{11,15},{16,20},{17,... | collective-permute-start | bytes 49160 | tf_op jit(solution)/shard_map/ppermute | solution.py:24
  77.1 1.4 collective-permute-done.13
  78.6 1.3 collective-permute-start.14
  79.9 4.5 %collective-permute-start.15 = (f32[6,1,512]{2,1,0:T(1,128)S(1)}, f32[6,1,512]{2,1,0:T(1,128)S(1)}, u32[]{:S(2)}, u32[]{:S(2)}) collective-permute-start(f32[6,1,512]{2,1,0:T(1,128)S(1)} %get-tuple-element.21), channel_id=1, source_target_pairs={{0,1},{1,2},{2,3},{4,5},{5,6},{6,7},{8,9},{9,10},{10,11},{12,13},{... | collective-permute-start | bytes 36872 | tf_op jit(solution)/shard_map/ppermute | solution.py:24
  84.4 1.4 collective-permute-done.15
  86.2 0.3 fusion.111
  86.6 21.9 %psum.29 = f32[256]{0:T(256)S(1)} all-reduce(f32[256]{0:T(256)S(1)} %reshape.215), channel_id=1, replica_groups=mesh['grp'=4,'gx'=2,'gy'=4] {'gx','gy'}, use_global_device_ids=true, to_apply=%region_1.2 | all-reduce | flops 256 | bytes 2048 | tf_op jit(solution)/shard_map/psum | solution.py:113
  108.5 0.3 fusion.139
  109.5 1.8 collective-permute-start.16
  111.3 1.3 collective-permute-start.17
  112.6 0.3 collective-permute-done.16
  112.8 4.2 %collective-permute-done.17 = f32[2,8,512]{2,1,0:T(8,128)S(1)} collective-permute-done((f32[2,8,512]{2,1,0:T(8,128)S(1)}, f32[2,8,512]{2,1,0:T(8,128)S(1)}, u32[]{:S(2)}, u32[]{:S(2)}) %collective-permute-start.17) | collective-permute-done | bytes 32800 | tf_op jit(solution)/shard_map/ppermute | solution.py:26
  117.1 1.6 collective-permute-start.18
  118.7 1.3 collective-permute-start.19
  120.0 0.3 collective-permute-done.18
  120.3 4.2 %collective-permute-done.19 = f32[8,2,512]{2,1,0:T(2,128)S(1)} collective-permute-done((f32[8,2,512]{2,1,0:T(2,128)S(1)}, f32[8,2,512]{2,1,0:T(2,128)S(1)}, u32[]{:S(2)}, u32[]{:S(2)}) %collective-permute-start.19) | collective-permute-done | bytes 32800 | tf_op jit(solution)/shard_map/ppermute | solution.py:26
  125.0 1.6 collective-permute-start.20
  126.6 1.3 collective-permute-start.21
  127.9 0.3 collective-permute-done.20
  128.2 4.2 %collective-permute-done.21 = f32[2,8,512]{2,1,0:T(8,128)S(1)} collective-permute-done((f32[2,8,512]{2,1,0:T(8,128)S(1)}, f32[2,8,512]{2,1,0:T(8,128)S(1)}, u32[]{:S(2)}, u32[]{:S(2)}) %collective-permute-start.21) | collective-permute-done | bytes 32800 | tf_op jit(solution)/shard_map/ppermute | solution.py:26
  132.4 1.9 collective-permute-start.22
  134.3 1.3 collective-permute-start.23
  135.6 0.3 collective-permute-done.22
  135.9 4.2 %collective-permute-done.23 = f32[8,2,512]{2,1,0:T(2,128)S(1)} collective-permute-done((f32[8,2,512]{2,1,0:T(2,128)S(1)}, f32[8,2,512]{2,1,0:T(2,128)S(1)}, u32[]{:S(2)}, u32[]{:S(2)}) %collective-permute-start.23) | collective-permute-done | bytes 32800 | tf_op jit(solution)/shard_map/ppermute | solution.py:26
  140.6 0.4 copy.39
  141.0 1.1 reshape.232
  142.1 6.7 %all_to_all.15 = f32[4,1,4096]{2,1,0:T(1,128)S(1)} all-to-all(f32[4,1,4096]{2,1,0:T(1,128)S(1)} %reshape.232), channel_id=1, replica_groups=mesh['grp'=4,'gx'=2,'gy'=4] {'grp'}, dimensions={0} | all-to-all | bytes 131072 | tf_op jit(solution)/shard_map/all_to_all | solution.py:123
  148.8 0.5 broadcast.290
  149.3 0.8 reduce.4
  150.1 1.3 reshape.233
  151.4 0.3 copy.40
  151.8 0.7 convolution_bitcast_fusion.6
  152.6 1.3 convolution_bitcast_fusion.7
  154.0 0.9 fusion.1
  154.9 0.9 copy.46
  155.8 39.5 %all-reduce.9 = (f32[32,4]{0,1:T(4,128)}, f32[64,4]{0,1:T(4,128)S(1)}) all-reduce(f32[32,4]{0,1:T(4,128)S(1)} %convolution_bitcast_fusion.6, f32[64,4]{0,1:T(4,128)S(1)} %convolution_bitcast_fusion.7), channel_id=1, replica_groups=mesh['grp'=4,'gx'=2,'gy'=4] {'grp','gx','gy'}, use_global_device_ids=true, to_apply=%region_2.3 | all-reduce | flops 384 | bytes 3072 | tf_op jit(solution)/shard_map/psum | solution.py:131
  195.3 0.9 convolution_add_fusion.1
  (83 shorter events, 4.5 us)
Async XLA Ops:
  0.6 27.4 %copy-start = (f32[256,256]{1,0:T(8,128)S(1)}, f32[256,256]{1,0:T(8,128)}, u32[]{:S(2)}) copy-start(f32[256,256]{1,0:T(8,128)} %param.13) | copy-start | bytes 786436
  29.0 3.8 %copy-start.1 = (f32[1,4,8,512]{3,2,1,0:T(8,128)S(1)}, f32[1,4,8,512]{3,2,1,0:T(8,128)}, u32[]{:S(2)}) copy-start(f32[1,4,8,512]{3,2,1,0:T(8,128)} %param.10) | copy-start | bytes 196612
  29.0 3.8 %copy-start.2 = (f32[4,8,512]{2,1,0:T(8,128)S(1)}, f32[4,8,512]{2,1,0:T(8,128)}, u32[]{:S(2)}) copy-start(f32[4,8,512]{2,1,0:T(8,128)} %param.11) | copy-start | bytes 196612
  29.0 9.9 %collective-permute-start = (f32[2,8,512]{2,1,0:T(8,128)S(1)}, f32[2,8,512]{2,1,0:T(8,128)S(1)}, u32[]{:S(2)}, u32[]{:S(2)}) collective-permute-start(f32[2,8,512]{2,1,0:T(8,128)S(1)} %get-tuple-element.30), channel_id=1, source_target_pairs={{0,4},{1,5},{2,6},{3,7},{8,12},{9,13},{10,14},{11,15},{16,20},{17,... | collective-permute-start | bytes 98312 | tf_op jit(solution)/shard_map/ppermute | solution.py:24
  31.5 7.4 %collective-permute-start.1 = (f32[2,8,512]{2,1,0:T(8,128)S(1)}, f32[2,8,512]{2,1,0:T(8,128)S(1)}, u32[]{:S(2)}, u32[]{:S(2)}) collective-permute-start(f32[2,8,512]{2,1,0:T(8,128)S(1)} %get-tuple-element.31), channel_id=1, source_target_pairs={{4,0},{5,1},{6,2},{7,3},{12,8},{13,9},{14,10},{15,11},{20,16},{21,... | collective-permute-start | bytes 98312 | tf_op jit(solution)/shard_map/ppermute | solution.py:26
  32.9 8.7 %collective-permute-start.4 = (f32[2,2,8,512]{3,2,1,0:T(8,128)S(1)}, f32[2,2,8,512]{3,2,1,0:T(8,128)S(1)}, u32[]{:S(2)}, u32[]{:S(2)}) collective-permute-start(f32[2,2,8,512]{3,2,1,0:T(8,128)S(1)} %get-tuple-element.16), channel_id=1, source_target_pairs={{0,4},{1,5},{2,6},{3,7},{8,12},{9,13},{10,14},{11,15},{16,20},{17,... | collective-permute-start | bytes 196616 | tf_op jit(solution)/shard_map/ppermute | solution.py:24
  37.4 6.2 %collective-permute-start.5 = (f32[2,2,8,512]{3,2,1,0:T(8,128)S(1)}, f32[2,2,8,512]{3,2,1,0:T(8,128)S(1)}, u32[]{:S(2)}, u32[]{:S(2)}) collective-permute-start(f32[2,2,8,512]{3,2,1,0:T(8,128)S(1)} %get-tuple-element.17), channel_id=1, source_target_pairs={{4,0},{5,1},{6,2},{7,3},{12,8},{13,9},{14,10},{15,11},{20,16},{21,... | collective-permute-start | bytes 196616 | tf_op jit(solution)/shard_map/ppermute | solution.py:26
  38.9 8.5 %collective-permute-start.2 = (f32[8,2,512]{2,1,0:T(2,128)S(1)}, f32[8,2,512]{2,1,0:T(2,128)S(1)}, u32[]{:S(2)}, u32[]{:S(2)}) collective-permute-start(f32[8,2,512]{2,1,0:T(2,128)S(1)} %get-tuple-element.18), channel_id=1, source_target_pairs={{0,1},{1,2},{2,3},{4,5},{5,6},{6,7},{8,9},{9,10},{10,11},{12,13},{... | collective-permute-start | bytes 98312 | tf_op jit(solution)/shard_map/ppermute | solution.py:24
  40.2 7.2 %collective-permute-start.3 = (f32[8,2,512]{2,1,0:T(2,128)S(1)}, f32[8,2,512]{2,1,0:T(2,128)S(1)}, u32[]{:S(2)}, u32[]{:S(2)}) collective-permute-start(f32[8,2,512]{2,1,0:T(2,128)S(1)} %get-tuple-element.19), channel_id=1, source_target_pairs={{1,0},{2,1},{3,2},{5,4},{6,5},{7,6},{9,8},{10,9},{11,10},{13,12},{... | collective-permute-start | bytes 98312 | tf_op jit(solution)/shard_map/ppermute | solution.py:26
  43.6 4.4 %collective-permute-start.6 = (f32[2,8,2,512]{3,2,1,0:T(2,128)S(1)}, f32[2,8,2,512]{3,2,1,0:T(2,128)S(1)}, u32[]{:S(2)}, u32[]{:S(2)}) collective-permute-start(f32[2,8,2,512]{3,2,1,0:T(2,128)S(1)} %get-tuple-element.8), channel_id=1, source_target_pairs={{0,1},{1,2},{2,3},{4,5},{5,6},{6,7},{8,9},{9,10},{10,11},{12,13},{... | collective-permute-start | bytes 196616 | tf_op jit(solution)/shard_map/ppermute | solution.py:24
  46.2 6.2 %collective-permute-start.7 = (f32[2,8,2,512]{3,2,1,0:T(2,128)S(1)}, f32[2,8,2,512]{3,2,1,0:T(2,128)S(1)}, u32[]{:S(2)}, u32[]{:S(2)}) collective-permute-start(f32[2,8,2,512]{3,2,1,0:T(2,128)S(1)} %get-tuple-element.9), channel_id=1, source_target_pairs={{1,0},{2,1},{3,2},{5,4},{6,5},{7,6},{9,8},{10,9},{11,10},{13,12},{... | collective-permute-start | bytes 196616 | tf_op jit(solution)/shard_map/ppermute | solution.py:26
  52.7 6.1 %collective-permute-start.8 = (f32[2,8,512]{2,1,0:T(8,128)S(1)}, f32[2,8,512]{2,1,0:T(8,128)S(1)}, u32[]{:S(2)}, u32[]{:S(2)}) collective-permute-start(f32[2,8,512]{2,1,0:T(8,128)S(1)} %get-tuple-element.28), channel_id=1, source_target_pairs={{0,4},{1,5},{2,6},{3,7},{8,12},{9,13},{10,14},{11,15},{16,20},{17,... | collective-permute-start | bytes 98312 | tf_op jit(solution)/shard_map/ppermute | solution.py:24
  57.3 5.8 %collective-permute-start.9 = (f32[2,8,512]{2,1,0:T(8,128)S(1)}, f32[2,8,512]{2,1,0:T(8,128)S(1)}, u32[]{:S(2)}, u32[]{:S(2)}) collective-permute-start(f32[2,8,512]{2,1,0:T(8,128)S(1)} %get-tuple-element.29), channel_id=1, source_target_pairs={{4,0},{5,1},{6,2},{7,3},{12,8},{13,9},{14,10},{15,11},{20,16},{21,... | collective-permute-start | bytes 98312 | tf_op jit(solution)/shard_map/ppermute | solution.py:26
  63.1 3.5 %collective-permute-start.10 = (f32[8,2,512]{2,1,0:T(2,128)S(1)}, f32[8,2,512]{2,1,0:T(2,128)S(1)}, u32[]{:S(2)}, u32[]{:S(2)}) collective-permute-start(f32[8,2,512]{2,1,0:T(2,128)S(1)} %get-tuple-element.14), channel_id=1, source_target_pairs={{0,1},{1,2},{2,3},{4,5},{5,6},{6,7},{8,9},{9,10},{10,11},{12,13},{... | collective-permute-start | bytes 98312 | tf_op jit(solution)/shard_map/ppermute | solution.py:24
  65.0 5.8 %collective-permute-start.11 = (f32[8,2,512]{2,1,0:T(2,128)S(1)}, f32[8,2,512]{2,1,0:T(2,128)S(1)}, u32[]{:S(2)}, u32[]{:S(2)}) collective-permute-start(f32[8,2,512]{2,1,0:T(2,128)S(1)} %get-tuple-element.15), channel_id=1, source_target_pairs={{1,0},{2,1},{3,2},{5,4},{6,5},{7,6},{9,8},{10,9},{11,10},{13,12},{... | collective-permute-start | bytes 98312 | tf_op jit(solution)/shard_map/ppermute | solution.py:26
  71.3 5.9 %collective-permute-start.12 = (f32[1,8,512]{2,1,0:T(8,128)S(1)}, f32[1,8,512]{2,1,0:T(8,128)S(1)}, u32[]{:S(2)}, u32[]{:S(2)}) collective-permute-start(f32[1,8,512]{2,1,0:T(8,128)S(1)} %get-tuple-element.27), channel_id=1, source_target_pairs={{4,0},{5,1},{6,2},{7,3},{12,8},{13,9},{14,10},{15,11},{20,16},{21,... | collective-permute-start | bytes 49160 | tf_op jit(solution)/shard_map/ppermute | solution.py:26
  72.6 6.0 %collective-permute-start.13 = (f32[1,8,512]{2,1,0:T(8,128)S(1)}, f32[1,8,512]{2,1,0:T(8,128)S(1)}, u32[]{:S(2)}, u32[]{:S(2)}) collective-permute-start(f32[1,8,512]{2,1,0:T(8,128)S(1)} %get-tuple-element.26), channel_id=1, source_target_pairs={{0,4},{1,5},{2,6},{3,7},{8,12},{9,13},{10,14},{11,15},{16,20},{17,... | collective-permute-start | bytes 49160 | tf_op jit(solution)/shard_map/ppermute | solution.py:24
  78.6 5.9 %collective-permute-start.14 = (f32[6,1,512]{2,1,0:T(1,128)S(1)}, f32[6,1,512]{2,1,0:T(1,128)S(1)}, u32[]{:S(2)}, u32[]{:S(2)}) collective-permute-start(f32[6,1,512]{2,1,0:T(1,128)S(1)} %get-tuple-element.20), channel_id=1, source_target_pairs={{1,0},{2,1},{3,2},{5,4},{6,5},{7,6},{9,8},{10,9},{11,10},{13,12},{... | collective-permute-start | bytes 36872 | tf_op jit(solution)/shard_map/ppermute | solution.py:26
  79.9 5.9 %collective-permute-start.15 = (f32[6,1,512]{2,1,0:T(1,128)S(1)}, f32[6,1,512]{2,1,0:T(1,128)S(1)}, u32[]{:S(2)}, u32[]{:S(2)}) collective-permute-start(f32[6,1,512]{2,1,0:T(1,128)S(1)} %get-tuple-element.21), channel_id=1, source_target_pairs={{0,1},{1,2},{2,3},{4,5},{5,6},{6,7},{8,9},{9,10},{10,11},{12,13},{... | collective-permute-start | bytes 36872 | tf_op jit(solution)/shard_map/ppermute | solution.py:24
  109.5 3.3 %collective-permute-start.16 = (f32[2,8,512]{2,1,0:T(8,128)S(1)}, f32[2,8,512]{2,1,0:T(8,128)S(1)}, u32[]{:S(2)}, u32[]{:S(2)}) collective-permute-start(f32[2,8,512]{2,1,0:T(8,128)S(1)} %get-tuple-element.24), channel_id=1, source_target_pairs={{0,4},{1,5},{2,6},{3,7},{8,12},{9,13},{10,14},{11,15},{16,20},{17,... | collective-permute-start | bytes 98312 | tf_op jit(solution)/shard_map/ppermute | solution.py:24
  111.3 5.8 %collective-permute-start.17 = (f32[2,8,512]{2,1,0:T(8,128)S(1)}, f32[2,8,512]{2,1,0:T(8,128)S(1)}, u32[]{:S(2)}, u32[]{:S(2)}) collective-permute-start(f32[2,8,512]{2,1,0:T(8,128)S(1)} %get-tuple-element.25), channel_id=1, source_target_pairs={{4,0},{5,1},{6,2},{7,3},{12,8},{13,9},{14,10},{15,11},{20,16},{21,... | collective-permute-start | bytes 98312 | tf_op jit(solution)/shard_map/ppermute | solution.py:26
  117.1 3.2 %collective-permute-start.18 = (f32[8,2,512]{2,1,0:T(2,128)S(1)}, f32[8,2,512]{2,1,0:T(2,128)S(1)}, u32[]{:S(2)}, u32[]{:S(2)}) collective-permute-start(f32[8,2,512]{2,1,0:T(2,128)S(1)} %get-tuple-element.12), channel_id=1, source_target_pairs={{0,1},{1,2},{2,3},{4,5},{5,6},{6,7},{8,9},{9,10},{10,11},{12,13},{... | collective-permute-start | bytes 98312 | tf_op jit(solution)/shard_map/ppermute | solution.py:24
  118.7 5.8 %collective-permute-start.19 = (f32[8,2,512]{2,1,0:T(2,128)S(1)}, f32[8,2,512]{2,1,0:T(2,128)S(1)}, u32[]{:S(2)}, u32[]{:S(2)}) collective-permute-start(f32[8,2,512]{2,1,0:T(2,128)S(1)} %get-tuple-element.13), channel_id=1, source_target_pairs={{1,0},{2,1},{3,2},{5,4},{6,5},{7,6},{9,8},{10,9},{11,10},{13,12},{... | collective-permute-start | bytes 98312 | tf_op jit(solution)/shard_map/ppermute | solution.py:26
  125.0 3.2 %collective-permute-start.20 = (f32[2,8,512]{2,1,0:T(8,128)S(1)}, f32[2,8,512]{2,1,0:T(8,128)S(1)}, u32[]{:S(2)}, u32[]{:S(2)}) collective-permute-start(f32[2,8,512]{2,1,0:T(8,128)S(1)} %get-tuple-element.22), channel_id=1, source_target_pairs={{0,4},{1,5},{2,6},{3,7},{8,12},{9,13},{10,14},{11,15},{16,20},{17,... | collective-permute-start | bytes 98312 | tf_op jit(solution)/shard_map/ppermute | solution.py:24
  126.6 5.8 %collective-permute-start.21 = (f32[2,8,512]{2,1,0:T(8,128)S(1)}, f32[2,8,512]{2,1,0:T(8,128)S(1)}, u32[]{:S(2)}, u32[]{:S(2)}) collective-permute-start(f32[2,8,512]{2,1,0:T(8,128)S(1)} %get-tuple-element.23), channel_id=1, source_target_pairs={{4,0},{5,1},{6,2},{7,3},{12,8},{13,9},{14,10},{15,11},{20,16},{21,... | collective-permute-start | bytes 98312 | tf_op jit(solution)/shard_map/ppermute | solution.py:26
  132.4 3.5 %collective-permute-start.22 = (f32[8,2,512]{2,1,0:T(2,128)S(1)}, f32[8,2,512]{2,1,0:T(2,128)S(1)}, u32[]{:S(2)}, u32[]{:S(2)}) collective-permute-start(f32[8,2,512]{2,1,0:T(2,128)S(1)} %get-tuple-element.10), channel_id=1, source_target_pairs={{0,1},{1,2},{2,3},{4,5},{5,6},{6,7},{8,9},{9,10},{10,11},{12,13},{... | collective-permute-start | bytes 98312 | tf_op jit(solution)/shard_map/ppermute | solution.py:24
  134.3 5.8 %collective-permute-start.23 = (f32[8,2,512]{2,1,0:T(2,128)S(1)}, f32[8,2,512]{2,1,0:T(2,128)S(1)}, u32[]{:S(2)}, u32[]{:S(2)}) collective-permute-start(f32[8,2,512]{2,1,0:T(2,128)S(1)} %get-tuple-element.11), channel_id=1, source_target_pairs={{1,0},{2,1},{3,2},{5,4},{6,5},{7,6},{9,8},{10,9},{11,10},{13,12},{... | collective-permute-start | bytes 98312 | tf_op jit(solution)/shard_map/ppermute | solution.py:26
  150.1 1.6 copy-start.4
  151.4 1.2 copy-start.3
  152.6 1.3 copy-start.5
  152.6 1.3 copy-start.7
  154.9 40.4 %copy-start.6 = (f32[64,64]{1,0:T(8,128)S(1)}, f32[64,64]{1,0:T(8,128)}, u32[]{:S(2)}) copy-start(f32[64,64]{1,0:T(8,128)} %param.19) | copy-start | bytes 49156
  155.8 39.5 %copy-start.8 = (f32[64,4]{0,1:T(4,128)S(1)}, f32[64,4]{0,1:T(4,128)}, u32[]{:S(2)}) copy-start(f32[64,4]{0,1:T(4,128)} %param.17) | copy-start | bytes 3076
where the time goes:
time: 197 us; the launch traced here: 196 us
  blocking collectives  91.4 us (46%)
  starting transfers between devices  48.8 us (25%)
  waiting for transfers between devices  36.6 us (19%)
  local copies, waits for them, and re-layouts  7.92 us (4%)
  matrix products  7.43 us (4%)
  other arithmetic  2.64 us (1%)
    psum x2, blocking collectives, body(): coarse_rhs = lax.psum(restrict(residual, maps), ('gx', 'gy'))  45.2 us
    psum x1, blocking collectives, body(): lax.psum((corange_part, core_part), ('grp', 'gx', 'gy'))  39.5 us
    ppermute x12, starting transfers between devices, with_halo(): lax.ppermute(tail, axis, [(i, (i + 1) % count) for i in range(ends)])  33.3 us
    ppermute x12, waiting for transfers between devices, with_halo(): lax.ppermute(head, axis, [((i + 1) % count, i) for i in range(ends)])  31.7 us
    ppermute x12, starting transfers between devices, with_halo(): lax.ppermute(head, axis, [((i + 1) % count, i) for i in range(ends)])  15.5 us
    all_to_all x1, blocking collectives, body(): lax.all_to_all(pressure[None], 'grp', split_axis=3, concat_axis=0, tiled=...  6.68 us
    ppermute x12, waiting for transfers between devices, with_halo(): lax.ppermute(tail, axis, [(i, (i + 1) % count) for i in range(ends)])  4.95 us
  transfers between devices with their start and end apart: 24, of which 17 were waited for; matrix products, arithmetic and copies ran while one was open for 0% of the time, Pallas kernels for 0%

commit v1 on v0

--- a/solution.py
+++ b/solution.py
@@ -1,16 +1,379 @@
+import functools
+
 import jax
 import jax.numpy as jnp
 from jax import lax
+from jax.experimental import pallas as pl
+from jax.experimental.pallas import tpu as pltpu
 from jax.sharding import PartitionSpec as P
 
 OUTER = 2
 SWEEPS = 4
 XY_CUTS = 4
 Z_CUTS = 16
-
+LANES = 128
+SUBLANES = 8
 
 jacobi_weight = 2.0 / 3.0
 highest = lax.Precision.HIGHEST
+
+
+def dot_nn(a, b):
+    return lax.dot_general(
+        a, b, (((1,), (0,)), ((), ())), precision=highest, preferred_element_type=jnp.float32
+    )
+
+
+def dot_nt(a, b):
+    return lax.dot_general(
+        a, b, (((1,), (1,)), ((), ())), precision=highest, preferred_element_type=jnp.float32
+    )
+
+
+def iota(shape, dim):
+    return lax.broadcasted_iota(jnp.int32, shape, dim)
+
+
+def spread_map(ids_ref, coarse):
+    cells_z = ids_ref.shape[2]
+    ranks = lax.bitwise_and(ids_ref[0, 0:1, :], Z_CUTS - 1)
+    rows = lax.bitwise_and(iota((coarse, cells_z), 0), Z_CUTS - 1)
+    return (rows == ranks).astype(jnp.float32)
+
+
+def column_map(ids_ref):
+    rows_x, rows_y, _ = ids_ref.shape
+    boxes = XY_CUTS * XY_CUTS
+    tile = ids_ref[:, :, :LANES].reshape(rows_x * rows_y, LANES) // Z_CUTS
+    turned = tile.astype(jnp.float32).T[:boxes]
+    return (turned == iota(turned.shape, 0).astype(jnp.float32)).astype(jnp.float32)
+
+
+def restrict(values, ids_ref, coarse):
+    boxes = XY_CUTS * XY_CUTS
+    by_box = dot_nn(column_map(ids_ref), values)
+    wide = dot_nt(by_box, spread_map(ids_ref, coarse))
+    own = iota((boxes, coarse), 1) // Z_CUTS == iota((boxes, coarse), 0)
+    return jnp.sum(jnp.where(own, wide, 0.0), axis=0, keepdims=True)
+
+
+def store_row(out_ref, row):
+    for part in range(row.shape[1] // LANES):
+        out_ref[part : part + 1, :] = row[:, part * LANES : (part + 1) * LANES]
+
+
+def begin_kernel(coarse, source_ref, ids_ref, out_ref):
+    rows_x, rows_y, cells_z = source_ref.shape
+    row = restrict(source_ref[...].reshape(rows_x * rows_y, cells_z), ids_ref, coarse)
+    store_row(out_ref, row)
+    lanes = iota((1, LANES), 1)
+    tile = ids_ref[:, :, :LANES] // Z_CUTS
+    ranks_x = tile[:, 0:1, :] // XY_CUTS
+    ranks_y = lax.bitwise_and(tile[0], XY_CUTS - 1)
+    below_x = jnp.sum((ranks_x <= lanes[None]).astype(jnp.float32), axis=0)
+    below_y = jnp.sum((ranks_y <= lanes - XY_CUTS).astype(jnp.float32), axis=0, keepdims=True)
+    last = coarse // LANES
+    out_ref[last : last + 1, :] = jnp.where(lanes < XY_CUTS, below_x, below_y)
+
+
+def coarse_planes(gathered, inverse_ref, ids_ref, scale_factor, cuts, place):
+    coarse = inverse_ref.shape[0]
+    boxes = XY_CUTS * XY_CUTS
+    _, cut_y = cuts
+    row = jnp.concatenate(
+        [gathered[part : part + 1, :] for part in range(coarse // LANES)], axis=1
+    )
+    row = jnp.broadcast_to(row * scale_factor, (SUBLANES, coarse))
+    solved = dot_nt(row, inverse_ref[...])[0:1]
+    own = iota((boxes, coarse), 1) // Z_CUTS == iota((boxes, coarse), 0)
+    along_z = dot_nn(jnp.where(own, solved, 0.0), spread_map(ids_ref, coarse))
+    place_y, inside = place
+    planes = []
+    for box_x in range(XY_CUTS):
+        first = box_x * XY_CUTS
+        plane = jnp.broadcast_to(along_z[first : first + 1], place_y.shape)
+        for box_y in range(1, XY_CUTS):
+            line = along_z[first + box_y : first + box_y + 1]
+            plane = jnp.where(place_y >= cut_y[box_y - 1], line, plane)
+        planes.append(jnp.where(inside, plane, 0.0))
+    return planes
+
+
+def correction_of(planes, cuts, place_x):
+    cut_x, _ = cuts
+    value = planes[0]
+    for box_x in range(1, XY_CUTS):
+        value = jnp.where(cut_x[box_x - 1] <= place_x, planes[box_x], value)
+    return value
+
+
+def cuts_of(row, count_x, count_y):
+    cut_x = [row[:, at : at + 1] * (1.0 / count_y) for at in range(XY_CUTS - 1)]
+    cut_y = [row[:, XY_CUTS + at : XY_CUTS + at + 1] * (1.0 / count_x) for at in range(XY_CUTS - 1)]
+    return cut_x, cut_y
+
+
+def beside_z(values):
+    cells_z = values.shape[-1]
+    lanes = iota(values.shape, values.ndim - 1)
+    ahead = pltpu.roll(values, cells_z - 1, values.ndim - 1)
+    behind = pltpu.roll(values, 1, values.ndim - 1)
+    return jnp.where(lanes == cells_z - 1, 0.0, ahead) + jnp.where(lanes == 0, 0.0, behind)
+
+
+def beside_y(values):
+    rows = values.shape[0]
+    return pltpu.roll(values, rows - 1, 0) + pltpu.roll(values, 1, 0)
+
+
+def neighbours(field_ref, at):
+    center = field_ref[at + 1]
+    return center, field_ref[at] + field_ref[at + 2] + beside_y(center) + beside_z(center)
+
+
+def sweep(from_ref, to_ref, weight_ref, drive_ref):
+    for at in range(weight_ref.shape[0]):
+        center, beside = neighbours(from_ref, at)
+        to_ref[at + 1] = (
+            center * (1.0 - jacobi_weight) + drive_ref[at] + weight_ref[at] * beside
+        )
+
+
+def window_place(count_y, rows_y, shape):
+    place_y = iota(shape, 0) + (lax.axis_index("gy") - 1) * rows_y
+    inside = (place_y >= 0) & (place_y < rows_y * count_y)
+    return place_y.astype(jnp.float32), inside
+
+
+def first_kernel(
+    counts, scale_factor, own_ref, other_ref, even_ref, even_other_ref, odd_ref, odd_other_ref,
+    ids_ref, inverse_ref, gathered_ref,
+    field_ref, weight_ref, drive_ref, out_ref, spare_ref,
+):
+    count_x, count_y = counts
+    _, rows_x, rows_y, cells_z = own_ref.shape
+    window_x, window_y, _ = weight_ref.shape
+    at_x, at_y = lax.axis_index("gx"), lax.axis_index("gy")
+    parity = lax.rem(at_y, 2)
+    even_row = pl.multiple_of((1 - parity) * 2 * rows_y, SUBLANES)
+    odd_row = pl.multiple_of(parity * 2 * rows_y, SUBLANES)
+    odd_inside = jnp.where((at_y > 0) & (at_y < count_y - 1), 1.0, 0.0)
+    own_x, other_x = at_x * rows_x, (1 - at_x) * rows_x
+    for ref, first_x, row, keep in (
+        (own_ref, own_x, rows_y, None),
+        (other_ref, other_x, rows_y, None),
+        (even_ref, own_x, even_row, None),
+        (even_other_ref, other_x, even_row, None),
+        (odd_ref, own_x, odd_row, odd_inside),
+        (odd_other_ref, other_x, odd_row, odd_inside),
+    ):
+        for at in range(rows_x):
+            weight = jacobi_weight / (6.0 + ref[1, at])
+            if keep is not None:
+                weight = weight * keep
+            weight_ref[first_x + at, pl.ds(row, rows_y), :] = weight
+            drive_ref[first_x + at, pl.ds(row, rows_y), :] = weight * ref[0, at]
+
+    gathered = jnp.sum(gathered_ref[...], axis=0)
+    coarse = inverse_ref.shape[0]
+    last = coarse // LANES
+    cuts = cuts_of(gathered[last : last + 1], count_x, count_y)
+    place = window_place(count_y, rows_y, (window_y, cells_z))
+    planes = coarse_planes(gathered, inverse_ref, ids_ref, scale_factor, cuts, place)
+    empty = jnp.zeros((window_y, cells_z), jnp.float32)
+    for ref in (field_ref, spare_ref):
+        ref[0] = empty
+        ref[window_x + 1] = empty
+    for at in range(window_x):
+        field_ref[at + 1] = correction_of(planes, cuts, float(at))
+    for step in range(SWEEPS // 2):
+        sweep(field_ref, spare_ref, weight_ref, drive_ref)
+        sweep(spare_ref, field_ref, weight_ref, drive_ref)
+
+    residual = []
+    for at in range(rows_x):
+        center, beside = neighbours(field_ref, own_x + at)
+        center, beside = center[rows_y : 2 * rows_y], beside[rows_y : 2 * rows_y]
+        residual.append(own_ref[0, at] - ((6.0 + own_ref[1, at]) * center - beside))
+    row = restrict(jnp.concatenate(residual, axis=0), ids_ref, coarse)
+    store_row(out_ref, row)
+    out_ref[last : last + 1, :] = gathered[last : last + 1]
+
+
+def second_kernel(
+    counts, scale_factor, pieces,
+    field_ref, weight_ref, drive_ref, ids_ref, inverse_ref, gathered_ref, *rest,
+):
+    out_refs, (one_ref, two_ref) = rest[:pieces], rest[pieces:]
+    count_x, count_y = counts
+    window_x, window_y, cells_z = weight_ref.shape
+    _, rows_y, chunk = out_refs[0].shape
+    rows_x = out_refs[0].shape[0]
+    own_x = lax.axis_index("gx") * rows_x
+    gathered = jnp.sum(gathered_ref[...], axis=0)
+    last = inverse_ref.shape[0] // LANES
+    cuts = cuts_of(gathered_ref[0, last : last + 1], count_x, count_y)
+    place = window_place(count_y, rows_y, (window_y, cells_z))
+    planes = coarse_planes(gathered, inverse_ref, ids_ref, scale_factor, cuts, place)
+    empty = jnp.zeros((window_y, cells_z), jnp.float32)
+    for ref in (one_ref, two_ref):
+        ref[0] = empty
+        ref[window_x + 1] = empty
+    for at in range(window_x):
+        one_ref[at + 1] = field_ref[at + 1] + correction_of(planes, cuts, float(at))
+    sweep(one_ref, two_ref, weight_ref, drive_ref)
+    for step in range(SWEEPS // 2 - 1):
+        sweep(two_ref, one_ref, weight_ref, drive_ref)
+        sweep(one_ref, two_ref, weight_ref, drive_ref)
+    for at in range(rows_x):
+        center, beside = neighbours(two_ref, own_x + at)
+        value = (
+            center * (1.0 - jacobi_weight)
+            + drive_ref[own_x + at]
+            + weight_ref[own_x + at] * beside
+        )
+        one_ref[at, pl.ds(0, rows_y), :] = value[rows_y : 2 * rows_y]
+    me = lax.axis_index("grp")
+    for turn in range(pieces):
+        first = pl.multiple_of(lax.bitwise_xor(me, turn) * chunk, LANES)
+        for at in range(rows_x):
+            out_refs[turn][at] = one_ref[at, pl.ds(0, rows_y), pl.ds(first, chunk)]
+
+
+def sketch_kernel(pieces, omega_ref, psi_ref, phi_ref, range_ref, *rest):
+    snaps, (new_ref, out_ref) = rest[:pieces], rest[pieces:]
+    rows_x = psi_ref.shape[1]
+    me = lax.axis_index("grp")
+    slots = [lax.bitwise_xor(me, turn) for turn in range(pieces)]
+    cells = [[snaps[turn][at] for at in range(rows_x)] for turn in range(pieces)]
+    corange, core = psi_ref.shape[0], phi_ref.shape[0]
+    ones = jnp.ones((SUBLANES, LANES), jnp.float32)
+    totals = [[] for _ in range(pieces)]
+    for ref, count in ((psi_ref, corange), (phi_ref, core)):
+        for at_row in range(count):
+            parts = [ref[at_row, at] for at in range(rows_x)]
+            for turn in range(pieces):
+                total = parts[0] * cells[turn][0]
+                for at in range(1, rows_x):
+                    total = total + parts[at] * cells[turn][at]
+                totals[turn].append(jnp.sum(total, axis=0, keepdims=True))
+    out_ref[...] = jnp.zeros_like(out_ref)
+    for turn in range(pieces):
+        row = dot_nt(ones, jnp.concatenate(totals[turn], axis=0))[0:1]
+        out_ref[pl.ds(slots[turn], 1), pl.ds(0, corange + core)] = row
+    for at_row in range(range_ref.shape[0]):
+        scales = [omega_ref[slots[turn], at_row] for turn in range(pieces)]
+        for at in range(rows_x):
+            value = range_ref[at_row, at]
+            for turn in range(pieces):
+                value = value + scales[turn] * cells[turn][at]
+            new_ref[at_row, at] = value
+
+
+def end_kernel(gathered_ref, xi_ref, core_ref, corange_out_ref, core_out_ref):
+    snaps = xi_ref.shape[1]
+    corange = corange_out_ref.shape[0]
+    core = core_ref.shape[0]
+    total = jnp.sum(gathered_ref[...], axis=0)
+    turned = jnp.concatenate([total, jnp.zeros((SUBLANES - snaps, LANES), jnp.float32)], axis=0).T
+    corange_out_ref[...] = turned[:corange, :snaps]
+    images = turned[corange : corange + core, :snaps]
+    core_out_ref[...] = core_ref[...] + dot_nt(images, xi_ref[...])
+
+
+vmem = pl.BlockSpec(memory_space=pltpu.VMEM)
+smem = pl.BlockSpec(memory_space=pltpu.SMEM)
+
+
+def call(kernel, outs, inputs, scratch=(), specs=None, name=None):
+    many = isinstance(outs, list)
+    shapes = [jax.ShapeDtypeStruct(shape, jnp.float32) for shape in (outs if many else [outs])]
+    result = pl.pallas_call(
+        kernel,
+        out_shape=shapes,
+        in_specs=specs or [vmem] * len(inputs),
+        out_specs=[vmem] * len(shapes),
+        scratch_shapes=[pltpu.VMEM(shape, jnp.float32) for shape in scratch],
+        name=name,
+    )(*inputs)
+    return result if many else result[0]
+
+
+def gather(values, axes, count):
+    copies = jnp.broadcast_to(values[None], (count,) + values.shape)
+    return lax.all_to_all(copies, axes, 0, 0)
+
+
+def fast_body(
+    sources, diagonal, coarse_ids, coarse_inverse, omega_rows, psi, phi, xi_cols, range_sketch,
+    core_sketch,
+):
+    source = sources[0]
+    rows_x, rows_y, cells_z = source.shape
+    counts = (lax.axis_size("gx"), lax.axis_size("gy"))
+    groups = lax.axis_size("grp")
+    count_x, count_y = counts
+    coarse = coarse_inverse.shape[0]
+    scale_factor = coarse / (rows_x * count_x * rows_y * count_y * cells_z)
+    window = (rows_x * count_x, 3 * rows_y, cells_z)
+    padded = (window[0] + 2,) + window[1:]
+    rows = coarse // LANES + 1
+
+    def partner_y(at, phase):
+        found = at ^ 1 if phase == 0 else ((at + 1) ^ 1) - 1
+        return found if 0 <= found < count_y else at
+
+    def pairs(cross, phase):
+        return [
+            (x * count_y + y, (x ^ cross) * count_y + (y if phase is None else partner_y(y, phase)))
+            for x in range(count_x)
+            for y in range(count_y)
+        ]
+
+    mine = jnp.stack([source, diagonal])
+    others = [
+        lax.ppermute(mine, ("gx", "gy"), pairs(cross, phase))
+        for cross, phase in ((1, None), (0, 0), (1, 0), (0, 1), (1, 1))
+    ]
+    begin = call(
+        functools.partial(begin_kernel, coarse), (rows, LANES), (source, coarse_ids), name="begin"
+    )
+    gathered = gather(begin, ("gx", "gy"), count_x * count_y)
+    field, weight, drive, partial = call(
+        functools.partial(first_kernel, counts, scale_factor),
+        [padded, window, window, (rows, LANES)],
+        (mine, *others, coarse_ids, coarse_inverse, gathered),
+        scratch=[padded],
+        name="first",
+    )
+    gathered = gather(partial, ("gx", "gy"), count_x * count_y)
+    chunk = cells_z // groups
+    pieces = call(
+        functools.partial(second_kernel, counts, scale_factor, groups),
+        [(rows_x, rows_y, chunk)] * groups,
+        (field, weight, drive, coarse_ids, coarse_inverse, gathered),
+        scratch=[padded, padded],
+        name="second",
+    )
+    snaps = [pieces[0]] + [
+        lax.ppermute(pieces[turn], "grp", [(at, at ^ turn) for at in range(groups)])
+        for turn in range(1, groups)
+    ]
+    range_new, products = call(
+        functools.partial(sketch_kernel, groups),
+        [range_sketch.shape, (groups, LANES)],
+        (omega_rows, psi, phi, range_sketch, *snaps),
+        specs=[smem] + [vmem] * (3 + groups),
+        name="sketch",
+    )
+    gathered = gather(products, ("grp", "gx", "gy"), groups * count_x * count_y)
+    corange_cols, core_new = call(
+        end_kernel,
+        [(psi.shape[0], groups), core_sketch.shape],
+        (gathered, xi_cols, core_sketch),
+        name="end",
+    )
+    return range_new, corange_cols, core_new
 
 
 def with_halo(cells, sides, width):
@@ -44,10 +407,6 @@
     return center + jacobi_weight * (source - applied) / (6.0 + diagonal)
 
 
-def widen_faces(values):
-    return with_halo(values, (("gx", 0), ("gy", 1)), 1)
-
-
 def axis_maps(coarse_ids):
     ranks_x = coarse_ids[:, 0, 0] // (XY_CUTS * Z_CUTS)
     ranks_y = coarse_ids[0, :, 0] // Z_CUTS % XY_CUTS
@@ -60,7 +419,7 @@
     return (map_x, map_y, map_z)
 
 
-def restrict(values, maps):
+def restrict_cells(values, maps):
     map_x, map_y, map_z = maps
     rows_x, rows_y, cells_z = values.shape
     along_z = jnp.dot(values.reshape(rows_x * rows_y, cells_z), map_z, precision=highest)
@@ -79,16 +438,8 @@
     return spread.reshape(extent)
 
 
-def body(
-    sources,
-    diagonal,
-    coarse_ids,
-    coarse_inverse,
-    omega_rows,
-    psi,
-    phi,
-    xi_cols,
-    range_sketch,
+def general_body(
+    sources, diagonal, coarse_ids, coarse_inverse, omega_rows, psi, phi, xi_cols, range_sketch,
     core_sketch,
 ):
     source = sources[0]
@@ -97,29 +448,18 @@
     total_cells = rows_x * lax.axis_size("gx") * rows_y * lax.axis_size("gy") * cells_z
     scale_factor = coarse / total_cells
     maps = axis_maps(coarse_ids)
-    stacked = jnp.stack([source, diagonal])
-    margin = with_halo(stacked, (("gx", 1), ("gy", 2)), 2)
-    place_x = lax.axis_index("gx") * rows_x + jnp.arange(rows_x + 4) - 2
-    place_y = lax.axis_index("gy") * rows_y + jnp.arange(rows_y + 4) - 2
-    inside_x = ((place_x >= 0) & (place_x < rows_x * lax.axis_size("gx"))).astype(jnp.float32)
-    inside_y = ((place_y >= 0) & (place_y < rows_y * lax.axis_size("gy"))).astype(jnp.float32)
-    inside = inside_x[:, None, None] * inside_y[None, :, None]
+    sides = (("gx", 0), ("gy", 1))
     pressure = jnp.zeros_like(source)
     for outer_step in range(OUTER):
         if outer_step == 0:
             residual = source
         else:
-            residual = source - neighbour_image(widen_faces(pressure), diagonal)[1]
-        coarse_rhs = lax.psum(restrict(residual, maps), ("gx", "gy"))
+            residual = source - neighbour_image(with_halo(pressure, sides, 1), diagonal)[1]
+        coarse_rhs = lax.psum(restrict_cells(residual, maps), ("gx", "gy"))
         correction = jnp.dot(coarse_inverse, coarse_rhs * scale_factor, precision=highest)
         pressure = pressure + prolong(correction, maps, source.shape)
-        for sweep_step in range(SWEEPS // 2):
-            widened = with_halo(pressure, (("gx", 0), ("gy", 1)), 2)
-            halfway = (
-                smooth_once(widened, margin[0, 1:-1, 1:-1], margin[1, 1:-1, 1:-1])
-                * inside[1:-1, 1:-1]
-            )
-            pressure = smooth_once(halfway, source, diagonal)
+        for sweep_step in range(SWEEPS):
+            pressure = smooth_once(with_halo(pressure, sides, 1), source, diagonal)
     snapshot = lax.all_to_all(pressure[None], "grp", split_axis=3, concat_axis=0, tiled=True)
     columns = snapshot.reshape(snapshot.shape[0], -1)
     range_flat = range_sketch.reshape(range_sketch.shape[0], -1)
@@ -131,6 +471,24 @@
     corange_cols, core_images = lax.psum((corange_part, core_part), ("grp", "gx", "gy"))
     core_new = core_sketch + jnp.dot(core_images, xi_cols.T, precision=highest)
     return (range_new.reshape(range_sketch.shape), corange_cols, core_new)
+
+
+def body(*arrays):
+    rows_x, rows_y, cells_z = arrays[1].shape
+    coarse, groups = arrays[3].shape[0], lax.axis_size("grp")
+    fits = (
+        lax.axis_size("gx") == 2
+        and lax.axis_size("gy") % 2 == 0
+        and rows_y >= OUTER * SWEEPS
+        and rows_y % SUBLANES == 0
+        and groups & (groups - 1) == 0
+        and groups <= SUBLANES
+        and cells_z % (groups * LANES) == 0
+        and cells_z // groups == LANES
+        and coarse % LANES == 0
+        and arrays[5].shape[0] + arrays[6].shape[0] <= LANES
+    )
+    return (fast_body if fits else general_body)(*arrays)
 
 
 def solution(mesh):

time: 197 us -> 70.1 us (0.36)
  blocking collectives: 91.4 us -> 22.7 us
  starting transfers between devices: 48.8 us -> 11.8 us
  waiting for transfers between devices: 36.6 us -> 9.65 us
  Pallas kernels: 0 us -> 16.3 us
  matrix products: 7.43 us -> 0 us
    psum x3 -> x0, blocking collectives: 84.7 us -> none  [the longest x2 45.2 us: body(): coarse_rhs = lax.psum(restrict(residual, maps), ('gx', 'gy'))]
    ppermute x24 -> x8, starting transfers between devices: 48.8 us -> 9.13 us  [the longest x5 7.27 us: fast_body(): lax.ppermute(mine, ('gx', 'gy'), pairs(cross, phase))]
    ppermute x24 -> x8, waiting for transfers between devices: 36.6 us -> 3.08 us  [the longest x3 3.07 us: fast_body(): lax.ppermute(pieces[turn], 'grp', [(at, at ^ turn) for at in range(groups)])]
    pallas_call x0 -> x5, Pallas kernels: none -> 16.3 us  [call(): pl.pallas_call(kernel, out_shape=shapes, in_specs=specs or [vmem] * len(i...]
    all_to_all x1 -> x2, blocking collectives: 6.68 us -> 22.7 us  [gather(): return lax.all_to_all(copies, axes, 0, 0)]
    dot_general x18 -> x0, matrix products: 7.43 us -> none  [the longest x1 1.32 us: body(): jnp.einsum('sc,tc->st', phi.reshape(phi.shape[0], -1), columns, precision...]
    all_to_all x0 -> x1, waiting for transfers between devices: none -> 6.57 us  [gather(): return lax.all_to_all(copies, axes, 0, 0)]
    all_to_all x0 -> x1, starting transfers between devices: none -> 2.67 us  [gather(): return lax.all_to_all(copies, axes, 0, 0)]
  transfers between devices with their start and end apart: 24 -> 9, of which waited for: 17 -> 3; matrix products, arithmetic and copies ran while one was open for 0% -> 2% of each run, Pallas kernels for 0% -> 3%
where the time goes in v1:
time: 70.1 us; the launch traced here: 69.5 us
  blocking collectives  22.7 us (32%)
  Pallas kernels  16.3 us (23%)
  starting transfers between devices  11.8 us (17%)
  waiting for transfers between devices  9.65 us (14%)
  local copies, waits for them, and re-layouts  7.37 us (11%)
  other arithmetic  0.88 us (1%)
  between operations  0.75 us (1%)
    all_to_all x2, blocking collectives, gather(): return lax.all_to_all(copies, axes, 0, 0)  22.7 us
    pallas_call x5, Pallas kernels, call(): pl.pallas_call(kernel, out_shape=shapes, in_specs=specs or [vmem] * len(i...  16.3 us
    ppermute x5, starting transfers between devices, fast_body(): lax.ppermute(mine, ('gx', 'gy'), pairs(cross, phase))  7.27 us
    all_to_all x1, waiting for transfers between devices, gather(): return lax.all_to_all(copies, axes, 0, 0)  6.57 us
    unnamed x24, local copies, waits for them, and re-layouts  4.69 us
    ppermute x3, waiting for transfers between devices, fast_body(): lax.ppermute(pieces[turn], 'grp', [(at, at ^ turn) for at in range(groups)])  3.07 us
    broadcast_in_dim x3, local copies, waits for them, and re-layouts, gather(): copies = jnp.broadcast_to(values[None], (count,) + values.shape)  2.68 us
    all_to_all x1, starting transfers between devices, gather(): return lax.all_to_all(copies, axes, 0, 0)  2.67 us
  transfers between devices with their start and end apart: 9, of which 3 were waited for; matrix products, arithmetic and copies ran while one was open for 2% of the time, Pallas kernels for 3%

profile of v1, /device:TPU:0, one launch (start us, length us, event | category | flops | bytes accessed | tf_op | source)
XLA Modules:
  0.0 69.5 jit_solution(4986505272606670132)
XLA Ops:
  0.6 0.9 %pad_maximum_fusion.own_ref = f32[2,4,8,512]{3,2,1,0:T(8,128)S(1)} fusion(f32[1,4,8,512]{3,2,1,0:T(8,128)} %bitcast.3, f32[1,4,8,512]{3,2,1,0:T(8,128)} %param.10), kind=kLoop, calls=%fused_computation | loop fusion | flops 32768 | bytes 262144 | tf_op jit(solution)/shard_map/stack | solution.py:333
  1.5 0.0 copy-start
  1.5 3.1 %collective-permute-start = (f32[2,4,8,512]{3,2,1,0:T(8,128)S(1)}, f32[2,4,8,512]{3,2,1,0:T(8,128)S(1)}, u32[]{:S(2)}, u32[]{:S(2)}) collective-permute-start(f32[2,4,8,512]{3,2,1,0:T(8,128)S(1)} %pad_maximum_fusion.own_ref), channel_id=1, source_target_pairs={{0,4},{1,5},{2,6},{3,7},{4,0},{5,1},{6,2},{7,3},{8,12},{9,13},{10,... | collective-permute-start | bytes 393224 | tf_op jit(solution)/shard_map/ppermute | solution.py:335
  4.6 1.6 %collective-permute-start.1 = (f32[2,4,8,512]{3,2,1,0:T(8,128)S(1)}, f32[2,4,8,512]{3,2,1,0:T(8,128)S(1)}, u32[]{:S(2)}, u32[]{:S(2)}) collective-permute-start(f32[2,4,8,512]{3,2,1,0:T(8,128)S(1)} %pad_maximum_fusion.own_ref), channel_id=1, source_target_pairs={{0,1},{1,0},{2,3},{3,2},{4,5},{5,4},{6,7},{7,6},{8,9},{9,8},{10,11... | collective-permute-start | bytes 393224 | tf_op jit(solution)/shard_map/ppermute | solution.py:335
  6.2 0.0 collective-permute-start.2
  6.2 0.7 collective-permute-start.3
  6.8 2.0 %collective-permute-start.4 = (f32[2,4,8,512]{3,2,1,0:T(8,128)S(1)}, f32[2,4,8,512]{3,2,1,0:T(8,128)S(1)}, u32[]{:S(2)}, u32[]{:S(2)}) collective-permute-start(f32[2,4,8,512]{3,2,1,0:T(8,128)S(1)} %pad_maximum_fusion.own_ref), channel_id=1, source_target_pairs={{0,4},{1,6},{2,5},{3,7},{4,0},{5,2},{6,1},{7,3},{8,12},{9,14},{10,... | collective-permute-start | bytes 393224 | tf_op jit(solution)/shard_map/ppermute | solution.py:335
  8.8 2.2 %begin.1 = f32[3,128]{1,0:T(4,128)} custom-call(f32[4,8,512]{2,1,0:T(8,128)} %bitcast.2, s32[4,8,512]{2,1,0:T(8,128)} %ids_ref.5), custom_call_target="tpu_custom_call" | custom-call | tf_op jit(solution)/shard_map/begin/pallas_call | solution.py:291
  11.0 0.7 broadcast_in_dim.6
  11.6 13.1 %all_to_all.15.gathered_ref = f32[8,3,128]{2,1,0:T(4,128)} all-to-all(f32[8,3,128]{2,1,0:T(4,128)S(1)} %broadcast_in_dim.6), channel_id=1, replica_groups=mesh['grp'=4,'gx'=2,'gy'=4] {'gx','gy'}, dimensions={0} | all-to-all | bytes 24576 | tf_op jit(solution)/shard_map/all_to_all | solution.py:304
  24.7 0.0 collective-permute-done.other_ref
  24.7 0.0 copy-start.2
  24.7 0.0 collective-permute-done.1.even_ref
  24.7 0.0 copy-start.3
  24.7 0.0 collective-permute-done.2.even_other_ref
  24.7 0.0 copy-start.4
  24.7 0.0 collective-permute-done.3.odd_ref
  24.8 0.0 copy-start.5
  24.8 0.0 collective-permute-done.4.odd_other_ref
  24.8 0.0 copy-done
  24.8 0.6 copy-done.2
  25.4 0.1 copy-done.3
  25.4 0.0 copy-done.4
  25.5 0.1 copy-done.5
  25.5 0.0 copy-start.6
  25.5 0.6 copy-done.6
  26.2 5.1 %first.1 = (f32[10,24,512]{2,1,0:T(8,128)}, f32[8,24,512]{2,1,0:T(8,128)}, f32[8,24,512]{2,1,0:T(8,128)}, f32[3,128]{1,0:T(4,128)}) custom-call(f32[2,4,8,512]{3,2,1,0:T(8,128)} %copy-done, f32[2,4,8,512]{3,2,1,0:T(8,128)} %copy-done.2, f32[2,4,8,512]{3,2,1,0:T(8,128)} %copy-done.3, f32[2,4,8,512]{3,2,1,0:T(8,128)} %copy-done.4, f32[2,4,8,512]{3,2,1,0:T(8,128)} %copy-done.5, ...), custom_call_target="tpu_custom_call" | custom-call | tf_op jit(solution)/shard_map/first/pallas_call | solution.py:291
  31.2 0.7 broadcast_in_dim.7
  31.9 9.6 %all_to_all.16.gathered_ref = f32[8,3,128]{2,1,0:T(4,128)} all-to-all(f32[8,3,128]{2,1,0:T(4,128)S(1)} %broadcast_in_dim.7), channel_id=1, replica_groups=mesh['grp'=4,'gx'=2,'gy'=4] {'gx','gy'}, dimensions={0} | all-to-all | bytes 24576 | tf_op jit(solution)/shard_map/all_to_all | solution.py:304
  41.6 3.9 %second.1 = (f32[4,8,128]{2,1,0:T(8,128)}, f32[4,8,128]{2,1,0:T(8,128)}, f32[4,8,128]{2,1,0:T(8,128)}, f32[4,8,128]{2,1,0:T(8,128)}) custom-call(f32[10,24,512]{2,1,0:T(8,128)} %get-tuple-element.15.field_ref, f32[8,24,512]{2,1,0:T(8,128)} %get-tuple-element.16.weight_ref, f32[8,24,512]{2,1,0:T(8,128)} %get-tuple-element.17.drive_ref, s32[4,8,512]{2,1,0:T(8,128)} %ids_ref.5, ...), custom_call_target="tpu_custom_call" | custom-call | tf_op jit(solution)/shard_map/second/pallas_call | solution.py:291
  45.5 0.0 collective-permute-start.5
  45.5 1.6 %collective-permute-start.6 = (f32[4,8,128]{2,1,0:T(8,128)}, f32[4,8,128]{2,1,0:T(8,128)S(1)}, u32[]{:S(2)}, u32[]{:S(2)}) collective-permute-start(f32[4,8,128]{2,1,0:T(8,128)} %get-tuple-element.21), channel_id=1, source_target_pairs={{0,16},{8,24},{16,0},{24,8},{1,17},{9,25},{17,1},{25,9},{2,18},{10... | collective-permute-start | bytes 49160 | tf_op jit(solution)/shard_map/ppermute | solution.py:359
  47.0 0.3 collective-permute-start.7
  47.3 0.0 collective-permute-done.5.rest_1_
  47.3 0.0 copy-start.7
  47.3 2.2 %collective-permute-done.6.rest_2_ = f32[4,8,128]{2,1,0:T(8,128)S(1)} collective-permute-done((f32[4,8,128]{2,1,0:T(8,128)}, f32[4,8,128]{2,1,0:T(8,128)S(1)}, u32[]{:S(2)}, u32[]{:S(2)}) %collective-permute-start.6) | collective-permute-done | bytes 16416 | tf_op jit(solution)/shard_map/ppermute | solution.py:359
  49.5 0.0 copy-start.8
  49.5 0.9 %collective-permute-done.7.rest_3_ = f32[4,8,128]{2,1,0:T(8,128)S(1)} collective-permute-done((f32[4,8,128]{2,1,0:T(8,128)}, f32[4,8,128]{2,1,0:T(8,128)S(1)}, u32[]{:S(2)}, u32[]{:S(2)}) %collective-permute-start.7) | collective-permute-done | bytes 16416 | tf_op jit(solution)/shard_map/ppermute | solution.py:359
  50.4 0.0 copy-start.9
  50.4 0.0 copy-done.7
  50.4 0.0 copy-done.8
  50.4 0.6 copy-done.9
  51.0 3.4 %sketch.1 = (f32[32,4,8,128]{3,2,1,0:T(8,128)}, f32[4,128]{1,0:T(4,128)}) custom-call(f32[4,32]{1,0:T(4,128)} %omega_ref.1, f32[32,4,8,128]{3,2,1,0:T(8,128)} %psi_ref.1, f32[64,4,8,128]{3,2,1,0:T(8,128)} %phi_ref.1, f32[32,4,8,128]{3,2,1,0:T(8,128)} %range_ref.1, f32[4,8,128]{2,1,0:T(8,128)} %get-tuple-element.19.rest_0_, f32[4,8,128]{2,1,0:T(8,128)} %copy-done.7, ...), custom_call_target="tpu_custom_call" | custom-call | tf_op jit(solution)/shard_map/sketch/pallas_call | solution.py:291
  54.5 1.3 %broadcast_in_dim.8 = f32[32,4,128]{2,1,0:T(4,128)} broadcast(f32[4,128]{1,0:T(4,128)} %get-tuple-element.24), dimensions={1,2} | broadcast | bytes 67584 | tf_op jit(solution)/shard_map/broadcast_in_dim | solution.py:303
  55.8 0.0 copy-start.10
  55.8 2.7 %all-to-all-start.2 = ((f32[32,4,128]{2,1,0:T(4,128)}), f32[32,4,128]{2,1,0:T(4,128)S(1)}, u32[]{:S(2)}, u32[]{:S(2)}) async-start(f32[32,4,128]{2,1,0:T(4,128)} %broadcast_in_dim.8), calls=%async_computation.2 | async-start | bytes 131072 | tf_op jit(solution)/shard_map/all_to_all | solution.py:304
  58.4 0.0 copy-done.10
  58.5 0.7 %copy.13.xi_ref = f32[64,4]{1,0:T(8,128)} copy(f32[64,4]{0,1:T(4,128)S(1)} %copy-done.10) | data formatting | bytes 2048 | tf_op args[7]
  59.2 6.6 %all-to-all-done.2.gathered_ref = f32[32,4,128]{2,1,0:T(4,128)S(1)} async-done(((f32[32,4,128]{2,1,0:T(4,128)}), f32[32,4,128]{2,1,0:T(4,128)S(1)}, u32[]{:S(2)}, u32[]{:S(2)}) %all-to-all-start.2) | async-done | bytes 65568 | tf_op jit(solution)/shard_map/all_to_all | solution.py:304
  65.7 0.0 copy-start.1
  65.7 0.6 copy-done.1
  66.3 1.8 %end.1 = (f32[32,4]{1,0:T(8,128)}, f32[64,64]{1,0:T(8,128)}) custom-call(f32[32,4,128]{2,1,0:T(4,128)} %copy-done.1, f32[64,4]{1,0:T(8,128)} %copy.13.xi_ref, f32[64,64]{1,0:T(8,128)} %core_ref.1), custom_call_target="tpu_custom_call" | custom-call | tf_op jit(solution)/shard_map/end/pallas_call | solution.py:291
  68.1 1.4 %copy.14 = f32[32,4]{0,1:T(4,128)} copy(f32[32,4]{1,0:T(8,128)} %get-tuple-element.28) | data formatting | bytes 1024
Async XLA Ops:
  1.5 23.3 %copy-start = (f32[2,4,8,512]{3,2,1,0:T(8,128)}, f32[2,4,8,512]{3,2,1,0:T(8,128)S(1)}, u32[]{:S(2)}) copy-start(f32[2,4,8,512]{3,2,1,0:T(8,128)S(1)} %pad_maximum_fusion.own_ref) | copy-start | bytes 393220
  1.5 23.2 %collective-permute-start = (f32[2,4,8,512]{3,2,1,0:T(8,128)S(1)}, f32[2,4,8,512]{3,2,1,0:T(8,128)S(1)}, u32[]{:S(2)}, u32[]{:S(2)}) collective-permute-start(f32[2,4,8,512]{3,2,1,0:T(8,128)S(1)} %pad_maximum_fusion.own_ref), channel_id=1, source_target_pairs={{0,4},{1,5},{2,6},{3,7},{4,0},{5,1},{6,2},{7,3},{8,12},{9,13},{10,... | collective-permute-start | bytes 393224 | tf_op jit(solution)/shard_map/ppermute | solution.py:335
  4.6 20.1 %collective-permute-start.1 = (f32[2,4,8,512]{3,2,1,0:T(8,128)S(1)}, f32[2,4,8,512]{3,2,1,0:T(8,128)S(1)}, u32[]{:S(2)}, u32[]{:S(2)}) collective-permute-start(f32[2,4,8,512]{3,2,1,0:T(8,128)S(1)} %pad_maximum_fusion.own_ref), channel_id=1, source_target_pairs={{0,1},{1,0},{2,3},{3,2},{4,5},{5,4},{6,7},{7,6},{8,9},{9,8},{10,11... | collective-permute-start | bytes 393224 | tf_op jit(solution)/shard_map/ppermute | solution.py:335
  6.2 18.6 %collective-permute-start.2 = (f32[2,4,8,512]{3,2,1,0:T(8,128)S(1)}, f32[2,4,8,512]{3,2,1,0:T(8,128)S(1)}, u32[]{:S(2)}, u32[]{:S(2)}) collective-permute-start(f32[2,4,8,512]{3,2,1,0:T(8,128)S(1)} %pad_maximum_fusion.own_ref), channel_id=1, source_target_pairs={{0,5},{1,4},{2,7},{3,6},{4,1},{5,0},{6,3},{7,2},{8,13},{9,12},{10,... | collective-permute-start | bytes 393224 | tf_op jit(solution)/shard_map/ppermute | solution.py:335
  6.2 18.6 %collective-permute-start.3 = (f32[2,4,8,512]{3,2,1,0:T(8,128)S(1)}, f32[2,4,8,512]{3,2,1,0:T(8,128)S(1)}, u32[]{:S(2)}, u32[]{:S(2)}) collective-permute-start(f32[2,4,8,512]{3,2,1,0:T(8,128)S(1)} %pad_maximum_fusion.own_ref), channel_id=1, source_target_pairs={{0,0},{1,2},{2,1},{3,3},{4,4},{5,6},{6,5},{7,7},{8,8},{9,10},{10,9... | collective-permute-start | bytes 393224 | tf_op jit(solution)/shard_map/ppermute | solution.py:335
  6.8 17.9 %collective-permute-start.4 = (f32[2,4,8,512]{3,2,1,0:T(8,128)S(1)}, f32[2,4,8,512]{3,2,1,0:T(8,128)S(1)}, u32[]{:S(2)}, u32[]{:S(2)}) collective-permute-start(f32[2,4,8,512]{3,2,1,0:T(8,128)S(1)} %pad_maximum_fusion.own_ref), channel_id=1, source_target_pairs={{0,4},{1,6},{2,5},{3,7},{4,0},{5,2},{6,1},{7,3},{8,12},{9,14},{10,... | collective-permute-start | bytes 393224 | tf_op jit(solution)/shard_map/ppermute | solution.py:335
  24.7 0.7 copy-start.2
  24.7 0.7 %copy-start.3 = (f32[2,4,8,512]{3,2,1,0:T(8,128)}, f32[2,4,8,512]{3,2,1,0:T(8,128)S(1)}, u32[]{:S(2)}) copy-start(f32[2,4,8,512]{3,2,1,0:T(8,128)S(1)} %collective-permute-done.1.even_ref) | copy-start | bytes 393220
  24.7 0.7 %copy-start.4 = (f32[2,4,8,512]{3,2,1,0:T(8,128)}, f32[2,4,8,512]{3,2,1,0:T(8,128)S(1)}, u32[]{:S(2)}) copy-start(f32[2,4,8,512]{3,2,1,0:T(8,128)S(1)} %collective-permute-done.2.even_other_ref) | copy-start | bytes 393220
  24.8 0.8 %copy-start.5 = (f32[2,4,8,512]{3,2,1,0:T(8,128)}, f32[2,4,8,512]{3,2,1,0:T(8,128)S(1)}, u32[]{:S(2)}) copy-start(f32[2,4,8,512]{3,2,1,0:T(8,128)S(1)} %collective-permute-done.3.odd_ref) | copy-start | bytes 393220
  25.5 0.6 copy-start.6
  45.5 1.9 %collective-permute-start.5 = (f32[4,8,128]{2,1,0:T(8,128)}, f32[4,8,128]{2,1,0:T(8,128)S(1)}, u32[]{:S(2)}, u32[]{:S(2)}) collective-permute-start(f32[4,8,128]{2,1,0:T(8,128)} %get-tuple-element.20), channel_id=1, source_target_pairs={{0,8},{8,0},{16,24},{24,16},{1,9},{9,1},{17,25},{25,17},{2,10},{10... | collective-permute-start | bytes 49160 | tf_op jit(solution)/shard_map/ppermute | solution.py:359
  45.5 4.0 %collective-permute-start.6 = (f32[4,8,128]{2,1,0:T(8,128)}, f32[4,8,128]{2,1,0:T(8,128)S(1)}, u32[]{:S(2)}, u32[]{:S(2)}) collective-permute-start(f32[4,8,128]{2,1,0:T(8,128)} %get-tuple-element.21), channel_id=1, source_target_pairs={{0,16},{8,24},{16,0},{24,8},{1,17},{9,25},{17,1},{25,9},{2,18},{10... | collective-permute-start | bytes 49160 | tf_op jit(solution)/shard_map/ppermute | solution.py:359
  47.0 3.4 %collective-permute-start.7 = (f32[4,8,128]{2,1,0:T(8,128)}, f32[4,8,128]{2,1,0:T(8,128)S(1)}, u32[]{:S(2)}, u32[]{:S(2)}) collective-permute-start(f32[4,8,128]{2,1,0:T(8,128)} %get-tuple-element.22), channel_id=1, source_target_pairs={{0,24},{8,16},{16,8},{24,0},{1,25},{9,17},{17,9},{25,1},{2,26},{10... | collective-permute-start | bytes 49160 | tf_op jit(solution)/shard_map/ppermute | solution.py:359
  47.3 3.1 %copy-start.7 = (f32[4,8,128]{2,1,0:T(8,128)}, f32[4,8,128]{2,1,0:T(8,128)S(1)}, u32[]{:S(2)}) copy-start(f32[4,8,128]{2,1,0:T(8,128)S(1)} %collective-permute-done.5.rest_1_) | copy-start | bytes 49156
  49.5 0.9 %copy-start.8 = (f32[4,8,128]{2,1,0:T(8,128)}, f32[4,8,128]{2,1,0:T(8,128)S(1)}, u32[]{:S(2)}) copy-start(f32[4,8,128]{2,1,0:T(8,128)S(1)} %collective-permute-done.6.rest_2_) | copy-start | bytes 49156
  50.4 0.6 copy-start.9
  55.8 2.7 %copy-start.10 = (f32[64,4]{0,1:T(4,128)S(1)}, f32[64,4]{0,1:T(4,128)}, u32[]{:S(2)}) copy-start(f32[64,4]{0,1:T(4,128)} %param.17) | copy-start | bytes 3076
  55.8 10.0 %all-to-all-start.2 = ((f32[32,4,128]{2,1,0:T(4,128)}), f32[32,4,128]{2,1,0:T(4,128)S(1)}, u32[]{:S(2)}, u32[]{:S(2)}) async-start(f32[32,4,128]{2,1,0:T(4,128)} %broadcast_in_dim.8), calls=%async_computation.2 | async-start | bytes 131072 | tf_op jit(solution)/shard_map/all_to_all | solution.py:304
  65.7 0.6 copy-start.1

commit v2 on v1

--- a/solution.py
+++ b/solution.py
@@ -13,6 +13,7 @@
 Z_CUTS = 16
 LANES = 128
 SUBLANES = 8
+VMEM_BYTES = 16 * 2**20
 
 jacobi_weight = 2.0 / 3.0
 highest = lax.Precision.HIGHEST
@@ -27,6 +28,12 @@
 def dot_nt(a, b):
     return lax.dot_general(
         a, b, (((1,), (1,)), ((), ())), precision=highest, preferred_element_type=jnp.float32
+    )
+
+
+def dot_tn(a, b):
+    return lax.dot_general(
+        a, b, (((0,), (0,)), ((), ())), precision=highest, preferred_element_type=jnp.float32
     )
 
 
@@ -57,23 +64,26 @@
     return jnp.sum(jnp.where(own, wide, 0.0), axis=0, keepdims=True)
 
 
-def store_row(out_ref, row):
-    for part in range(row.shape[1] // LANES):
-        out_ref[part : part + 1, :] = row[:, part * LANES : (part + 1) * LANES]
+def store_copies(out_ref, rows):
+    for copy in range(out_ref.shape[0]):
+        for at, row in enumerate(rows):
+            out_ref[copy, at : at + 1, :] = row
+
+
+def lane_rows(row):
+    return [row[:, at : at + LANES] for at in range(0, row.shape[1], LANES)]
 
 
 def begin_kernel(coarse, source_ref, ids_ref, out_ref):
     rows_x, rows_y, cells_z = source_ref.shape
     row = restrict(source_ref[...].reshape(rows_x * rows_y, cells_z), ids_ref, coarse)
-    store_row(out_ref, row)
     lanes = iota((1, LANES), 1)
     tile = ids_ref[:, :, :LANES] // Z_CUTS
     ranks_x = tile[:, 0:1, :] // XY_CUTS
     ranks_y = lax.bitwise_and(tile[0], XY_CUTS - 1)
     below_x = jnp.sum((ranks_x <= lanes[None]).astype(jnp.float32), axis=0)
     below_y = jnp.sum((ranks_y <= lanes - XY_CUTS).astype(jnp.float32), axis=0, keepdims=True)
-    last = coarse // LANES
-    out_ref[last : last + 1, :] = jnp.where(lanes < XY_CUTS, below_x, below_y)
+    store_copies(out_ref, lane_rows(row) + [jnp.where(lanes < XY_CUTS, below_x, below_y)])
 
 
 def coarse_planes(gathered, inverse_ref, ids_ref, scale_factor, cuts, place):
@@ -196,8 +206,7 @@
         center, beside = center[rows_y : 2 * rows_y], beside[rows_y : 2 * rows_y]
         residual.append(own_ref[0, at] - ((6.0 + own_ref[1, at]) * center - beside))
     row = restrict(jnp.concatenate(residual, axis=0), ids_ref, coarse)
-    store_row(out_ref, row)
-    out_ref[last : last + 1, :] = gathered[last : last + 1]
+    store_copies(out_ref, lane_rows(row) + [gathered[last : last + 1]])
 
 
 def second_kernel(
@@ -257,10 +266,11 @@
                 for at in range(1, rows_x):
                     total = total + parts[at] * cells[turn][at]
                 totals[turn].append(jnp.sum(total, axis=0, keepdims=True))
-    out_ref[...] = jnp.zeros_like(out_ref)
+    rest = jnp.zeros((LANES - corange - core, LANES), jnp.float32)
     for turn in range(pieces):
-        row = dot_nt(ones, jnp.concatenate(totals[turn], axis=0))[0:1]
-        out_ref[pl.ds(slots[turn], 1), pl.ds(0, corange + core)] = row
+        row = dot_nt(ones, jnp.concatenate(totals[turn] + [rest], axis=0))[0:1]
+        for copy in range(out_ref.shape[0]):
+            out_ref[copy, pl.ds(slots[turn], 1), :] = row
     for at_row in range(range_ref.shape[0]):
         scales = [omega_ref[slots[turn], at_row] for turn in range(pieces)]
         for at in range(rows_x):
@@ -271,14 +281,12 @@
 
 
 def end_kernel(gathered_ref, xi_ref, core_ref, corange_out_ref, core_out_ref):
-    snaps = xi_ref.shape[1]
-    corange = corange_out_ref.shape[0]
+    corange = corange_out_ref.shape[1]
     core = core_ref.shape[0]
     total = jnp.sum(gathered_ref[...], axis=0)
-    turned = jnp.concatenate([total, jnp.zeros((SUBLANES - snaps, LANES), jnp.float32)], axis=0).T
-    corange_out_ref[...] = turned[:corange, :snaps]
-    images = turned[corange : corange + core, :snaps]
-    core_out_ref[...] = core_ref[...] + dot_nt(images, xi_ref[...])
+    corange_out_ref[...] = total[:, :corange]
+    images = total[:, corange : corange + core]
+    core_out_ref[...] = core_ref[...] + dot_tn(images, xi_ref[...])
 
 
 vmem = pl.BlockSpec(memory_space=pltpu.VMEM)
@@ -294,13 +302,13 @@
         in_specs=specs or [vmem] * len(inputs),
         out_specs=[vmem] * len(shapes),
         scratch_shapes=[pltpu.VMEM(shape, jnp.float32) for shape in scratch],
+        compiler_params=pltpu.CompilerParams(vmem_limit_bytes=VMEM_BYTES),
         name=name,
     )(*inputs)
     return result if many else result[0]
 
 
-def gather(values, axes, count):
-    copies = jnp.broadcast_to(values[None], (count,) + values.shape)
+def gather(copies, axes):
     return lax.all_to_all(copies, axes, 0, 0)
 
 
@@ -317,7 +325,7 @@
     scale_factor = coarse / (rows_x * count_x * rows_y * count_y * cells_z)
     window = (rows_x * count_x, 3 * rows_y, cells_z)
     padded = (window[0] + 2,) + window[1:]
-    rows = coarse // LANES + 1
+    copies = (count_x * count_y, coarse // LANES + 1, LANES)
 
     def partner_y(at, phase):
         found = at ^ 1 if phase == 0 else ((at + 1) ^ 1) - 1
@@ -336,17 +344,17 @@
         for cross, phase in ((1, None), (0, 0), (1, 0), (0, 1), (1, 1))
     ]
     begin = call(
-        functools.partial(begin_kernel, coarse), (rows, LANES), (source, coarse_ids), name="begin"
-    )
-    gathered = gather(begin, ("gx", "gy"), count_x * count_y)
+        functools.partial(begin_kernel, coarse), copies, (source, coarse_ids), name="begin"
+    )
+    gathered = gather(begin, ("gx", "gy"))
     field, weight, drive, partial = call(
         functools.partial(first_kernel, counts, scale_factor),
-        [padded, window, window, (rows, LANES)],
+        [padded, window, window, copies],
         (mine, *others, coarse_ids, coarse_inverse, gathered),
         scratch=[padded],
         name="first",
     )
-    gathered = gather(partial, ("gx", "gy"), count_x * count_y)
+    gathered = gather(partial, ("gx", "gy"))
     chunk = cells_z // groups
     pieces = call(
         functools.partial(second_kernel, counts, scale_factor, groups),
@@ -361,19 +369,19 @@
     ]
     range_new, products = call(
         functools.partial(sketch_kernel, groups),
-        [range_sketch.shape, (groups, LANES)],
+        [range_sketch.shape, (groups * count_x * count_y, groups, LANES)],
         (omega_rows, psi, phi, range_sketch, *snaps),
         specs=[smem] + [vmem] * (3 + groups),
         name="sketch",
     )
-    gathered = gather(products, ("grp", "gx", "gy"), groups * count_x * count_y)
+    gathered = gather(products, ("grp", "gx", "gy"))
     corange_cols, core_new = call(
         end_kernel,
-        [(psi.shape[0], groups), core_sketch.shape],
-        (gathered, xi_cols, core_sketch),
+        [(groups, psi.shape[0]), core_sketch.shape],
+        (gathered, xi_cols.T, core_sketch),
         name="end",
     )
-    return range_new, corange_cols, core_new
+    return range_new, corange_cols.T, core_new
 
 
 def with_halo(cells, sides, width):

time: 70.1 us -> 56.3 us (0.80)
  Pallas kernels: 16.3 us -> 9.33 us
  waiting for transfers between devices: 9.65 us -> 2.89 us
  blocking collectives: 22.7 us -> 28.9 us
  local copies, waits for them, and re-layouts: 7.37 us -> 1.72 us
    pallas_call x5, Pallas kernels: 16.3 us -> 9.33 us  [call(): pl.pallas_call(kernel, out_shape=shapes, in_specs=specs or [vmem] * len(i...]
    all_to_all x1 -> x0, waiting for transfers between devices: 6.57 us -> none  [gather(): return lax.all_to_all(copies, axes, 0, 0)]
    all_to_all x2 -> x3, blocking collectives: 22.7 us -> 28.9 us  [gather(): return lax.all_to_all(copies, axes, 0, 0)]
    unnamed x24 -> x20, local copies, waits for them, and re-layouts: 4.69 us -> 1.72 us
    broadcast_in_dim x3 -> x0, local copies, waits for them, and re-layouts: 2.68 us -> none  [gather(): copies = jnp.broadcast_to(values[None], (count,) + values.shape)]
    all_to_all x1 -> x0, starting transfers between devices: 2.67 us -> none  [gather(): return lax.all_to_all(copies, axes, 0, 0)]
    ppermute x5, starting transfers between devices: 7.27 us -> 9.53 us  [fast_body(): lax.ppermute(mine, ('gx', 'gy'), pairs(cross, phase))]
  transfers between devices with their start and end apart: 9 -> 8, of which waited for: 3 -> 2; matrix products, arithmetic and copies ran while one was open for 2% -> 0% of each run, Pallas kernels for 3% -> 1%
where the time goes in v2:
time: 56.3 us; the launch traced here: 55.9 us
  blocking collectives  28.9 us (51%)
  starting transfers between devices  11.4 us (20%)
  Pallas kernels  9.33 us (17%)
  waiting for transfers between devices  2.89 us (5%)
  local copies, waits for them, and re-layouts  1.72 us (3%)
  other arithmetic  0.92 us (2%)
  between operations  0.76 us (1%)
    all_to_all x3, blocking collectives, gather(): return lax.all_to_all(copies, axes, 0, 0)  28.9 us
    ppermute x5, starting transfers between devices, fast_body(): lax.ppermute(mine, ('gx', 'gy'), pairs(cross, phase))  9.53 us
    pallas_call x5, Pallas kernels, call(): pl.pallas_call(kernel, out_shape=shapes, in_specs=specs or [vmem] * len(i...  9.33 us
    ppermute x3, waiting for transfers between devices, fast_body(): lax.ppermute(pieces[turn], 'grp', [(at, at ^ turn) for at in range(groups)])  2.88 us
    ppermute x3, starting transfers between devices, fast_body(): lax.ppermute(pieces[turn], 'grp', [(at, at ^ turn) for at in range(groups)])  1.91 us
    unnamed x20, local copies, waits for them, and re-layouts  1.72 us
  transfers between devices with their start and end apart: 8, of which 2 were waited for; matrix products, arithmetic and copies ran while one was open for 0% of the time, Pallas kernels for 1%

profile of v2, /device:TPU:0, one launch (start us, length us, event | category | flops | bytes accessed | tf_op | source)
XLA Modules:
  0.0 55.9 jit_solution(14691808784340751699)
XLA Ops:
  0.6 0.0 copy-start
  0.6 0.9 %pad_maximum_fusion.own_ref = f32[2,4,8,512]{3,2,1,0:T(8,128)S(1)} fusion(f32[1,4,8,512]{3,2,1,0:T(8,128)} %bitcast.6, f32[1,4,8,512]{3,2,1,0:T(8,128)} %param.10), kind=kLoop, calls=%fused_computation | loop fusion | flops 32768 | bytes 262144 | tf_op jit(solution)/shard_map/stack | solution.py:341
  1.6 3.1 %collective-permute-start.4 = (f32[2,4,8,512]{3,2,1,0:T(8,128)S(1)}, f32[2,4,8,512]{3,2,1,0:T(8,128)S(1)}, u32[]{:S(2)}, u32[]{:S(2)}) collective-permute-start(f32[2,4,8,512]{3,2,1,0:T(8,128)S(1)} %pad_maximum_fusion.own_ref), channel_id=1, source_target_pairs={{0,4},{1,6},{2,5},{3,7},{4,0},{5,2},{6,1},{7,3},{8,12},{9,14},{10,... | collective-permute-start | bytes 393224 | tf_op jit(solution)/shard_map/ppermute | solution.py:343
  4.6 0.7 %collective-permute-start.3 = (f32[2,4,8,512]{3,2,1,0:T(8,128)S(1)}, f32[2,4,8,512]{3,2,1,0:T(8,128)S(1)}, u32[]{:S(2)}, u32[]{:S(2)}) collective-permute-start(f32[2,4,8,512]{3,2,1,0:T(8,128)S(1)} %pad_maximum_fusion.own_ref), channel_id=1, source_target_pairs={{0,0},{1,2},{2,1},{3,3},{4,4},{5,6},{6,5},{7,7},{8,8},{9,10},{10,9... | collective-permute-start | bytes 393224 | tf_op jit(solution)/shard_map/ppermute | solution.py:343
  5.3 4.3 %collective-permute-start.2 = (f32[2,4,8,512]{3,2,1,0:T(8,128)S(1)}, f32[2,4,8,512]{3,2,1,0:T(8,128)S(1)}, u32[]{:S(2)}, u32[]{:S(2)}) collective-permute-start(f32[2,4,8,512]{3,2,1,0:T(8,128)S(1)} %pad_maximum_fusion.own_ref), channel_id=1, source_target_pairs={{0,5},{1,4},{2,7},{3,6},{4,1},{5,0},{6,3},{7,2},{8,13},{9,12},{10,... | collective-permute-start | bytes 393224 | tf_op jit(solution)/shard_map/ppermute | solution.py:343
  9.6 0.1 collective-permute-start.1
  9.7 1.4 %collective-permute-start = (f32[2,4,8,512]{3,2,1,0:T(8,128)S(1)}, f32[2,4,8,512]{3,2,1,0:T(8,128)S(1)}, u32[]{:S(2)}, u32[]{:S(2)}) collective-permute-start(f32[2,4,8,512]{3,2,1,0:T(8,128)S(1)} %pad_maximum_fusion.own_ref), channel_id=1, source_target_pairs={{0,4},{1,5},{2,6},{3,7},{4,0},{5,1},{6,2},{7,3},{8,12},{9,13},{10,... | collective-permute-start | bytes 393224 | tf_op jit(solution)/shard_map/ppermute | solution.py:343
  11.1 0.0 copy-start.2
  11.1 0.8 %copy-done.2 = s32[4,8,512]{2,1,0:T(8,128)S(1)} copy-done((s32[4,8,512]{2,1,0:T(8,128)S(1)}, s32[4,8,512]{2,1,0:T(8,128)}, u32[]{:S(2)}) %copy-start.2) | copy-done | bytes 65560
  11.9 0.0 copy-start.6
  11.9 0.8 %copy-done.6 = f32[1,4,8,512]{3,2,1,0:T(8,128)S(1)} copy-done((f32[1,4,8,512]{3,2,1,0:T(8,128)S(1)}, f32[1,4,8,512]{3,2,1,0:T(8,128)}, u32[]{:S(2)}) %copy-start.6) | copy-done | bytes 65560
  12.8 0.0 copy-start.3
  12.8 0.7 %begin.1 = f32[8,3,128]{2,1,0:T(4,128)S(1)} custom-call(f32[4,8,512]{2,1,0:T(8,128)S(1)} %bitcast.4, s32[4,8,512]{2,1,0:T(8,128)S(1)} %copy-done.2), custom_call_target="tpu_custom_call" | custom-call | tf_op jit(solution)/shard_map/begin/pallas_call | solution.py:299
  13.5 10.7 %all_to_all.15.gathered_ref = f32[8,3,128]{2,1,0:T(4,128)S(1)} all-to-all(f32[8,3,128]{2,1,0:T(4,128)S(1)} %begin.1), channel_id=1, replica_groups=mesh['grp'=4,'gx'=2,'gy'=4] {'gx','gy'}, dimensions={0} | all-to-all | bytes 24576 | tf_op jit(solution)/shard_map/all_to_all | solution.py:312
  24.2 0.0 collective-permute-done.4.odd_other_ref
  24.2 0.0 collective-permute-done.3.odd_ref
  24.2 0.0 collective-permute-done.2.even_other_ref
  24.2 0.0 collective-permute-done.1.even_ref
  24.2 0.0 collective-permute-done.other_ref
  24.2 0.0 copy-done
  24.3 0.0 copy-done.3
  24.3 0.0 copy-start.5
  24.3 3.2 %first.1 = (f32[10,24,512]{2,1,0:T(8,128)S(1)}, f32[8,24,512]{2,1,0:T(8,128)S(1)}, f32[8,24,512]{2,1,0:T(8,128)S(1)}, f32[8,3,128]{2,1,0:T(4,128)S(1)}) custom-call(f32[2,4,8,512]{3,2,1,0:T(8,128)S(1)} %pad_maximum_fusion.own_ref, f32[2,4,8,512]{3,2,1,0:T(8,128)S(1)} %collective-permute-done.other_ref, f32[2,4,8,512]{3,2,1,0:T(8,128)S(1)} %collective-permute-done.1.even_ref, ...), custom_call_target="tpu_custom_call" | custom-call | tf_op jit(solution)/shard_map/first/pallas_call | solution.py:299
  27.5 0.0 copy-start.1
  27.5 9.1 %all_to_all.16.gathered_ref = f32[8,3,128]{2,1,0:T(4,128)S(1)} all-to-all(f32[8,3,128]{2,1,0:T(4,128)S(1)} %get-tuple-element.18), channel_id=1, replica_groups=mesh['grp'=4,'gx'=2,'gy'=4] {'gx','gy'}, dimensions={0} | all-to-all | bytes 24576 | tf_op jit(solution)/shard_map/all_to_all | solution.py:312
  36.6 0.0 copy-start.4
  36.6 2.0 %second.1 = (f32[4,8,128]{2,1,0:T(8,128)S(1)}, f32[4,8,128]{2,1,0:T(8,128)S(1)}, f32[4,8,128]{2,1,0:T(8,128)S(1)}, f32[4,8,128]{2,1,0:T(8,128)S(1)}) custom-call(f32[10,24,512]{2,1,0:T(8,128)S(1)} %get-tuple-element.15.field_ref, f32[8,24,512]{2,1,0:T(8,128)S(1)} %get-tuple-element.16.weight_ref, f32[8,24,512]{2,1,0:T(8,128)S(1)} %get-tuple-element.17.drive_ref, ...), custom_call_target="tpu_custom_call" | custom-call | tf_op jit(solution)/shard_map/second/pallas_call | solution.py:299
  38.6 0.1 collective-permute-start.5
  38.7 0.0 copy-start.8
  38.7 1.6 %collective-permute-start.6 = (f32[4,8,128]{2,1,0:T(8,128)S(1)}, f32[4,8,128]{2,1,0:T(8,128)S(1)}, u32[]{:S(2)}, u32[]{:S(2)}) collective-permute-start(f32[4,8,128]{2,1,0:T(8,128)S(1)} %get-tuple-element.21), channel_id=1, source_target_pairs={{0,16},{8,24},{16,0},{24,8},{1,17},{9,25},{17,1},{25,9},{2,18},{10... | collective-permute-start | bytes 49160 | tf_op jit(solution)/shard_map/ppermute | solution.py:367
  40.2 0.3 collective-permute-start.7
  40.5 0.0 collective-permute-done.5.rest_1_
  40.5 2.0 %collective-permute-done.6.rest_2_ = f32[4,8,128]{2,1,0:T(8,128)S(1)} collective-permute-done((f32[4,8,128]{2,1,0:T(8,128)S(1)}, f32[4,8,128]{2,1,0:T(8,128)S(1)}, u32[]{:S(2)}, u32[]{:S(2)}) %collective-permute-start.6) | collective-permute-done | bytes 16416 | tf_op jit(solution)/shard_map/ppermute | solution.py:367
  42.5 0.9 %collective-permute-done.7.rest_3_ = f32[4,8,128]{2,1,0:T(8,128)S(1)} collective-permute-done((f32[4,8,128]{2,1,0:T(8,128)S(1)}, f32[4,8,128]{2,1,0:T(8,128)S(1)}, u32[]{:S(2)}, u32[]{:S(2)}) %collective-permute-start.7) | collective-permute-done | bytes 16416 | tf_op jit(solution)/shard_map/ppermute | solution.py:367
  43.4 0.0 copy-done.5
  43.4 0.0 copy-done.1
  43.4 0.0 copy-done.4
  43.4 0.0 copy-done.8
  43.4 2.5 %sketch.1 = (f32[32,4,8,128]{3,2,1,0:T(8,128)}, f32[32,4,128]{2,1,0:T(4,128)S(1)}) custom-call(f32[4,32]{1,0:T(4,128)S(1)} %copy-done.8, f32[32,4,8,128]{3,2,1,0:T(8,128)S(1)} %copy-done.4, f32[64,4,8,128]{3,2,1,0:T(8,128)S(1)} %copy-done.1, f32[32,4,8,128]{3,2,1,0:T(8,128)S(1)} %copy-done.5, f32[4,8,128]{2,1,0:T(8,128)S(1)} %get-tuple-element.19.rest_0_, ...), custom_call_target="tpu_custom_call" | custom-call | tf_op jit(solution)/shard_map/sketch/pallas_call | solution.py:299
  45.9 0.0 copy-start.7
  45.9 0.0 copy-start.9
  45.9 9.1 %all_to_all.17.gathered_ref = f32[32,4,128]{2,1,0:T(4,128)S(1)} all-to-all(f32[32,4,128]{2,1,0:T(4,128)S(1)} %get-tuple-element.24), channel_id=1, replica_groups=mesh['grp'=4,'gx'=2,'gy'=4] {'grp','gx','gy'}, dimensions={0} | all-to-all | bytes 131072 | tf_op jit(solution)/shard_map/all_to_all | solution.py:312
  55.0 0.0 copy-done.7
  55.0 0.0 copy-done.9
  55.0 0.9 %end.1 = (f32[4,32]{1,0:T(4,128)}, f32[64,64]{1,0:T(8,128)}) custom-call(f32[32,4,128]{2,1,0:T(4,128)S(1)} %all_to_all.17.gathered_ref, f32[4,64]{1,0:T(4,128)S(1)} %bitcast.5, f32[64,64]{1,0:T(8,128)S(1)} %copy-done.7), custom_call_target="tpu_custom_call" | custom-call | tf_op jit(solution)/shard_map/end/pallas_call | solution.py:299
Async XLA Ops:
  0.6 23.6 %copy-start = (f32[256,256]{1,0:T(8,128)S(1)}, f32[256,256]{1,0:T(8,128)}, u32[]{:S(2)}) copy-start(f32[256,256]{1,0:T(8,128)} %inverse_ref.3) | copy-start | bytes 786436
  1.6 22.6 %collective-permute-start.4 = (f32[2,4,8,512]{3,2,1,0:T(8,128)S(1)}, f32[2,4,8,512]{3,2,1,0:T(8,128)S(1)}, u32[]{:S(2)}, u32[]{:S(2)}) collective-permute-start(f32[2,4,8,512]{3,2,1,0:T(8,128)S(1)} %pad_maximum_fusion.own_ref), channel_id=1, source_target_pairs={{0,4},{1,6},{2,5},{3,7},{4,0},{5,2},{6,1},{7,3},{8,12},{9,14},{10,... | collective-permute-start | bytes 393224 | tf_op jit(solution)/shard_map/ppermute | solution.py:343
  4.6 19.6 %collective-permute-start.3 = (f32[2,4,8,512]{3,2,1,0:T(8,128)S(1)}, f32[2,4,8,512]{3,2,1,0:T(8,128)S(1)}, u32[]{:S(2)}, u32[]{:S(2)}) collective-permute-start(f32[2,4,8,512]{3,2,1,0:T(8,128)S(1)} %pad_maximum_fusion.own_ref), channel_id=1, source_target_pairs={{0,0},{1,2},{2,1},{3,3},{4,4},{5,6},{6,5},{7,7},{8,8},{9,10},{10,9... | collective-permute-start | bytes 393224 | tf_op jit(solution)/shard_map/ppermute | solution.py:343
  5.3 18.9 %collective-permute-start.2 = (f32[2,4,8,512]{3,2,1,0:T(8,128)S(1)}, f32[2,4,8,512]{3,2,1,0:T(8,128)S(1)}, u32[]{:S(2)}, u32[]{:S(2)}) collective-permute-start(f32[2,4,8,512]{3,2,1,0:T(8,128)S(1)} %pad_maximum_fusion.own_ref), channel_id=1, source_target_pairs={{0,5},{1,4},{2,7},{3,6},{4,1},{5,0},{6,3},{7,2},{8,13},{9,12},{10,... | collective-permute-start | bytes 393224 | tf_op jit(solution)/shard_map/ppermute | solution.py:343
  9.6 14.6 %collective-permute-start.1 = (f32[2,4,8,512]{3,2,1,0:T(8,128)S(1)}, f32[2,4,8,512]{3,2,1,0:T(8,128)S(1)}, u32[]{:S(2)}, u32[]{:S(2)}) collective-permute-start(f32[2,4,8,512]{3,2,1,0:T(8,128)S(1)} %pad_maximum_fusion.own_ref), channel_id=1, source_target_pairs={{0,1},{1,0},{2,3},{3,2},{4,5},{5,4},{6,7},{7,6},{8,9},{9,8},{10,11... | collective-permute-start | bytes 393224 | tf_op jit(solution)/shard_map/ppermute | solution.py:343
  9.7 14.5 %collective-permute-start = (f32[2,4,8,512]{3,2,1,0:T(8,128)S(1)}, f32[2,4,8,512]{3,2,1,0:T(8,128)S(1)}, u32[]{:S(2)}, u32[]{:S(2)}) collective-permute-start(f32[2,4,8,512]{3,2,1,0:T(8,128)S(1)} %pad_maximum_fusion.own_ref), channel_id=1, source_target_pairs={{0,4},{1,5},{2,6},{3,7},{4,0},{5,1},{6,2},{7,3},{8,12},{9,13},{10,... | collective-permute-start | bytes 393224 | tf_op jit(solution)/shard_map/ppermute | solution.py:343
  11.1 0.8 %copy-start.2 = (s32[4,8,512]{2,1,0:T(8,128)S(1)}, s32[4,8,512]{2,1,0:T(8,128)}, u32[]{:S(2)}) copy-start(s32[4,8,512]{2,1,0:T(8,128)} %ids_ref.5) | copy-start | bytes 196612
  11.9 0.8 %copy-start.6 = (f32[1,4,8,512]{3,2,1,0:T(8,128)S(1)}, f32[1,4,8,512]{3,2,1,0:T(8,128)}, u32[]{:S(2)}) copy-start(f32[1,4,8,512]{3,2,1,0:T(8,128)} %param.10) | copy-start | bytes 196612
  12.8 11.5 %copy-start.3 = (s32[4,8,512]{2,1,0:T(8,128)S(1)}, s32[4,8,512]{2,1,0:T(8,128)}, u32[]{:S(2)}) copy-start(s32[4,8,512]{2,1,0:T(8,128)} %ids_ref.5) | copy-start | bytes 196612
  24.3 19.1 %copy-start.5 = (f32[32,4,8,128]{3,2,1,0:T(8,128)S(1)}, f32[32,4,8,128]{3,2,1,0:T(8,128)}, u32[]{:S(2)}) copy-start(f32[32,4,8,128]{3,2,1,0:T(8,128)} %range_ref.1) | copy-start | bytes 1572868
  27.5 15.9 %copy-start.1 = (f32[64,4,8,128]{3,2,1,0:T(8,128)S(1)}, f32[64,4,8,128]{3,2,1,0:T(8,128)}, u32[]{:S(2)}) copy-start(f32[64,4,8,128]{3,2,1,0:T(8,128)} %phi_ref.1) | copy-start | bytes 3145732
  36.6 6.8 %copy-start.4 = (f32[32,4,8,128]{3,2,1,0:T(8,128)S(1)}, f32[32,4,8,128]{3,2,1,0:T(8,128)}, u32[]{:S(2)}) copy-start(f32[32,4,8,128]{3,2,1,0:T(8,128)} %psi_ref.1) | copy-start | bytes 1572868
  38.6 1.9 %collective-permute-start.5 = (f32[4,8,128]{2,1,0:T(8,128)S(1)}, f32[4,8,128]{2,1,0:T(8,128)S(1)}, u32[]{:S(2)}, u32[]{:S(2)}) collective-permute-start(f32[4,8,128]{2,1,0:T(8,128)S(1)} %get-tuple-element.20), channel_id=1, source_target_pairs={{0,8},{8,0},{16,24},{24,16},{1,9},{9,1},{17,25},{25,17},{2,10},{10... | collective-permute-start | bytes 49160 | tf_op jit(solution)/shard_map/ppermute | solution.py:367
  38.7 4.7 %copy-start.8 = (f32[4,32]{1,0:T(4,128)S(1)}, f32[4,32]{1,0:T(4,128)}, u32[]{:S(2)}) copy-start(f32[4,32]{1,0:T(4,128)} %omega_ref.1) | copy-start | bytes 1540
  38.7 3.8 %collective-permute-start.6 = (f32[4,8,128]{2,1,0:T(8,128)S(1)}, f32[4,8,128]{2,1,0:T(8,128)S(1)}, u32[]{:S(2)}, u32[]{:S(2)}) collective-permute-start(f32[4,8,128]{2,1,0:T(8,128)S(1)} %get-tuple-element.21), channel_id=1, source_target_pairs={{0,16},{8,24},{16,0},{24,8},{1,17},{9,25},{17,1},{25,9},{2,18},{10... | collective-permute-start | bytes 49160 | tf_op jit(solution)/shard_map/ppermute | solution.py:367
  40.2 3.2 %collective-permute-start.7 = (f32[4,8,128]{2,1,0:T(8,128)S(1)}, f32[4,8,128]{2,1,0:T(8,128)S(1)}, u32[]{:S(2)}, u32[]{:S(2)}) collective-permute-start(f32[4,8,128]{2,1,0:T(8,128)S(1)} %get-tuple-element.22), channel_id=1, source_target_pairs={{0,24},{8,16},{16,8},{24,0},{1,25},{9,17},{17,9},{25,1},{2,26},{10... | collective-permute-start | bytes 49160 | tf_op jit(solution)/shard_map/ppermute | solution.py:367
  45.9 9.1 %copy-start.7 = (f32[64,64]{1,0:T(8,128)S(1)}, f32[64,64]{1,0:T(8,128)}, u32[]{:S(2)}) copy-start(f32[64,64]{1,0:T(8,128)} %core_ref.1) | copy-start | bytes 49156
  45.9 9.1 %copy-start.9 = (f32[64,4]{0,1:T(4,128)S(1)}, f32[64,4]{0,1:T(4,128)}, u32[]{:S(2)}) copy-start(f32[64,4]{0,1:T(4,128)} %param.17) | copy-start | bytes 3076

commit v3 on v2

--- a/solution.py
+++ b/solution.py
@@ -6,6 +6,7 @@
 from jax.experimental import pallas as pl
 from jax.experimental.pallas import tpu as pltpu
 from jax.sharding import PartitionSpec as P
+
 
 OUTER = 2
 SWEEPS = 4
@@ -74,9 +75,28 @@
     return [row[:, at : at + LANES] for at in range(0, row.shape[1], LANES)]
 
 
-def begin_kernel(coarse, source_ref, ids_ref, out_ref):
-    rows_x, rows_y, cells_z = source_ref.shape
-    row = restrict(source_ref[...].reshape(rows_x * rows_y, cells_z), ids_ref, coarse)
+def begin_kernel(
+    source_from, diagonal_from, ids_from, inverse_from,
+    mine_ref, ids_ref, inverse_ref, out_ref, arrived,
+):
+    loads = [
+        pltpu.make_async_copy(source, target, arrived.at[at])
+        for at, (source, target) in enumerate(
+            (
+                (ids_from, ids_ref),
+                (source_from, mine_ref.at[0]),
+                (diagonal_from, mine_ref.at[1]),
+                (inverse_from, inverse_ref),
+            )
+        )
+    ]
+    for load in loads:
+        load.start()
+    coarse = inverse_ref.shape[0]
+    rows_x, rows_y, cells_z = ids_ref.shape
+    loads[0].wait()
+    loads[1].wait()
+    row = restrict(mine_ref[0].reshape(rows_x * rows_y, cells_z), ids_ref, coarse)
     lanes = iota((1, LANES), 1)
     tile = ids_ref[:, :, :LANES] // Z_CUTS
     ranks_x = tile[:, 0:1, :] // XY_CUTS
@@ -84,6 +104,8 @@
     below_x = jnp.sum((ranks_x <= lanes[None]).astype(jnp.float32), axis=0)
     below_y = jnp.sum((ranks_y <= lanes - XY_CUTS).astype(jnp.float32), axis=0, keepdims=True)
     store_copies(out_ref, lane_rows(row) + [jnp.where(lanes < XY_CUTS, below_x, below_y)])
+    loads[2].wait()
+    loads[3].wait()
 
 
 def coarse_planes(gathered, inverse_ref, ids_ref, scale_factor, cuts, place):
@@ -196,7 +218,7 @@
         ref[window_x + 1] = empty
     for at in range(window_x):
         field_ref[at + 1] = correction_of(planes, cuts, float(at))
-    for step in range(SWEEPS // 2):
+    for _ in range(SWEEPS // 2):
         sweep(field_ref, spare_ref, weight_ref, drive_ref)
         sweep(spare_ref, field_ref, weight_ref, drive_ref)
 
@@ -231,7 +253,7 @@
     for at in range(window_x):
         one_ref[at + 1] = field_ref[at + 1] + correction_of(planes, cuts, float(at))
     sweep(one_ref, two_ref, weight_ref, drive_ref)
-    for step in range(SWEEPS // 2 - 1):
+    for _ in range(SWEEPS // 2 - 1):
         sweep(two_ref, one_ref, weight_ref, drive_ref)
         sweep(one_ref, two_ref, weight_ref, drive_ref)
     for at in range(rows_x):
@@ -249,8 +271,23 @@
             out_refs[turn][at] = one_ref[at, pl.ds(0, rows_y), pl.ds(first, chunk)]
 
 
-def sketch_kernel(pieces, omega_ref, psi_ref, phi_ref, range_ref, *rest):
-    snaps, (new_ref, out_ref) = rest[:pieces], rest[pieces:]
+def range_kernel(pieces, omega_ref, range_ref, *rest):
+    snaps, (new_ref,) = rest[:pieces], rest[pieces:]
+    rows_x = range_ref.shape[1]
+    me = lax.axis_index("grp")
+    slots = [lax.bitwise_xor(me, turn) for turn in range(pieces)]
+    cells = [[snaps[turn][at] for at in range(rows_x)] for turn in range(pieces)]
+    for at_row in range(range_ref.shape[0]):
+        scales = [omega_ref[slots[turn], at_row] for turn in range(pieces)]
+        for at in range(rows_x):
+            value = range_ref[at_row, at]
+            for turn in range(pieces):
+                value = value + scales[turn] * cells[turn][at]
+            new_ref[at_row, at] = value
+
+
+def sketch_kernel(pieces, psi_ref, phi_ref, *rest):
+    snaps, (out_ref,) = rest[:pieces], rest[pieces:]
     rows_x = psi_ref.shape[1]
     me = lax.axis_index("grp")
     slots = [lax.bitwise_xor(me, turn) for turn in range(pieces)]
@@ -271,13 +308,6 @@
         row = dot_nt(ones, jnp.concatenate(totals[turn] + [rest], axis=0))[0:1]
         for copy in range(out_ref.shape[0]):
             out_ref[copy, pl.ds(slots[turn], 1), :] = row
-    for at_row in range(range_ref.shape[0]):
-        scales = [omega_ref[slots[turn], at_row] for turn in range(pieces)]
-        for at in range(rows_x):
-            value = range_ref[at_row, at]
-            for turn in range(pieces):
-                value = value + scales[turn] * cells[turn][at]
-            new_ref[at_row, at] = value
 
 
 def end_kernel(gathered_ref, xi_ref, core_ref, corange_out_ref, core_out_ref):
@@ -293,7 +323,7 @@
 smem = pl.BlockSpec(memory_space=pltpu.SMEM)
 
 
-def call(kernel, outs, inputs, scratch=(), specs=None, name=None):
+def call(kernel, outs, inputs, scratch=(), specs=None):
     many = isinstance(outs, list)
     shapes = [jax.ShapeDtypeStruct(shape, jnp.float32) for shape in (outs if many else [outs])]
     result = pl.pallas_call(
@@ -303,9 +333,12 @@
         out_specs=[vmem] * len(shapes),
         scratch_shapes=[pltpu.VMEM(shape, jnp.float32) for shape in scratch],
         compiler_params=pltpu.CompilerParams(vmem_limit_bytes=VMEM_BYTES),
-        name=name,
     )(*inputs)
     return result if many else result[0]
+
+
+def in_hbm(array):
+    return pltpu.with_memory_space_constraint(array, pltpu.HBM)
 
 
 def gather(copies, axes):
@@ -338,48 +371,57 @@
             for y in range(count_y)
         ]
 
-    mine = jnp.stack([source, diagonal])
+    mine, ids, inverse, begin = pl.pallas_call(
+        begin_kernel,
+        out_shape=[
+            jax.ShapeDtypeStruct((2,) + source.shape, jnp.float32),
+            jax.ShapeDtypeStruct(coarse_ids.shape, jnp.int32),
+            jax.ShapeDtypeStruct(coarse_inverse.shape, jnp.float32),
+            jax.ShapeDtypeStruct(copies, jnp.float32),
+        ],
+        in_specs=[pl.BlockSpec(memory_space=pltpu.HBM)] * 4,
+        out_specs=[vmem] * 4,
+        scratch_shapes=[pltpu.SemaphoreType.DMA((4,))],
+        compiler_params=pltpu.CompilerParams(vmem_limit_bytes=VMEM_BYTES),
+        name="begin",
+    )(*map(in_hbm, (source, diagonal, coarse_ids, coarse_inverse)))
+    gathered = gather(begin, ("gx", "gy"))
     others = [
         lax.ppermute(mine, ("gx", "gy"), pairs(cross, phase))
         for cross, phase in ((1, None), (0, 0), (1, 0), (0, 1), (1, 1))
     ]
-    begin = call(
-        functools.partial(begin_kernel, coarse), copies, (source, coarse_ids), name="begin"
-    )
-    gathered = gather(begin, ("gx", "gy"))
     field, weight, drive, partial = call(
         functools.partial(first_kernel, counts, scale_factor),
         [padded, window, window, copies],
-        (mine, *others, coarse_ids, coarse_inverse, gathered),
+        (mine, *others, ids, inverse, gathered),
         scratch=[padded],
-        name="first",
     )
     gathered = gather(partial, ("gx", "gy"))
     chunk = cells_z // groups
     pieces = call(
         functools.partial(second_kernel, counts, scale_factor, groups),
         [(rows_x, rows_y, chunk)] * groups,
-        (field, weight, drive, coarse_ids, coarse_inverse, gathered),
+        (field, weight, drive, ids, inverse, gathered),
         scratch=[padded, padded],
-        name="second",
     )
     snaps = [pieces[0]] + [
         lax.ppermute(pieces[turn], "grp", [(at, at ^ turn) for at in range(groups)])
         for turn in range(1, groups)
     ]
-    range_new, products = call(
+    products = call(
         functools.partial(sketch_kernel, groups),
-        [range_sketch.shape, (groups * count_x * count_y, groups, LANES)],
-        (omega_rows, psi, phi, range_sketch, *snaps),
-        specs=[smem] + [vmem] * (3 + groups),
-        name="sketch",
+        (groups * count_x * count_y, groups, LANES),
+        (psi, phi, *snaps),
     )
     gathered = gather(products, ("grp", "gx", "gy"))
+    range_new = call(
+        functools.partial(range_kernel, groups),
+        range_sketch.shape,
+        (omega_rows, range_sketch, *snaps),
+        specs=[smem] + [vmem] * (1 + groups),
+    )
     corange_cols, core_new = call(
-        end_kernel,
-        [(groups, psi.shape[0]), core_sketch.shape],
-        (gathered, xi_cols.T, core_sketch),
-        name="end",
+        end_kernel, [(groups, psi.shape[0]), core_sketch.shape], (gathered, xi_cols.T, core_sketch)
     )
     return range_new, corange_cols.T, core_new
 
@@ -466,7 +508,7 @@
         coarse_rhs = lax.psum(restrict_cells(residual, maps), ("gx", "gy"))
         correction = jnp.dot(coarse_inverse, coarse_rhs * scale_factor, precision=highest)
         pressure = pressure + prolong(correction, maps, source.shape)
-        for sweep_step in range(SWEEPS):
+        for _ in range(SWEEPS):
             pressure = smooth_once(with_halo(pressure, sides, 1), source, diagonal)
     snapshot = lax.all_to_all(pressure[None], "grp", split_axis=3, concat_axis=0, tiled=True)
     columns = snapshot.reshape(snapshot.shape[0], -1)
@@ -482,7 +524,7 @@
 
 
 def body(*arrays):
-    rows_x, rows_y, cells_z = arrays[1].shape
+    _, rows_y, cells_z = arrays[1].shape
     coarse, groups = arrays[3].shape[0], lax.axis_size("grp")
     fits = (
         lax.axis_size("gx") == 2
@@ -496,7 +538,9 @@
         and coarse % LANES == 0
         and arrays[5].shape[0] + arrays[6].shape[0] <= LANES
     )
-    return (fast_body if fits else general_body)(*arrays)
+    if not fits:
+        return general_body(*arrays)
+    return fast_body(*arrays)
 
 
 def solution(mesh):

time: 56.3 us -> 54.5 us (0.968)
  blocking collectives: 28.9 us -> 19.8 us
  waiting for transfers between devices: 2.89 us -> 8.59 us
  starting transfers between devices: 11.4 us -> 14.1 us
  local copies, waits for them, and re-layouts: 1.72 us -> 0.03 us
  Pallas kernels: 9.33 us -> 11 us
  other arithmetic: 0.92 us -> 0 us
    all_to_all x3 -> x2, blocking collectives: 28.9 us -> 19.8 us  [gather(): return lax.all_to_all(copies, axes, 0, 0)]
    all_to_all x0 -> x1, waiting for transfers between devices: none -> 5.7 us  [gather(): return lax.all_to_all(copies, axes, 0, 0)]
    all_to_all x0 -> x1, starting transfers between devices: none -> 2.69 us  [gather(): return lax.all_to_all(copies, axes, 0, 0)]
    unnamed x20 -> x12, local copies, waits for them, and re-layouts: 1.72 us -> 0.03 us
    pallas_call x0 -> x1, Pallas kernels: none -> 1.63 us  [fast_body(): pl.pallas_call(begin_kernel, out_shape=[jax.ShapeDtypeStruct((2,) + sourc...]
    another operation x1 -> x0, other arithmetic: 0.92 us -> none  [fast_body(): mine = jnp.stack([source, diagonal])]
  transfers between devices with their start and end apart: 8 -> 9, of which waited for: 2 -> 3; matrix products, arithmetic and copies ran while one was open for 0% -> 0% of each run, Pallas kernels for 1% -> 3%
where the time goes in v3:
time: 54.5 us; the launch traced here: 54.2 us
  blocking collectives  19.8 us (36%)
  starting transfers between devices  14.1 us (26%)
  Pallas kernels  11 us (20%)
  waiting for transfers between devices  8.59 us (16%)
  between operations  0.74 us (1%)
    all_to_all x2, blocking collectives, gather(): return lax.all_to_all(copies, axes, 0, 0)  19.8 us
    ppermute x5, starting transfers between devices, fast_body(): lax.ppermute(mine, ('gx', 'gy'), pairs(cross, phase))  9.53 us
    pallas_call x5, Pallas kernels, call(): pl.pallas_call(kernel, out_shape=shapes, in_specs=specs or [vmem] * len(i...  9.33 us
    all_to_all x1, waiting for transfers between devices, gather(): return lax.all_to_all(copies, axes, 0, 0)  5.7 us
    ppermute x3, waiting for transfers between devices, fast_body(): lax.ppermute(pieces[turn], 'grp', [(at, at ^ turn) for at in range(groups)])  2.87 us
    all_to_all x1, starting transfers between devices, gather(): return lax.all_to_all(copies, axes, 0, 0)  2.69 us
    ppermute x3, starting transfers between devices, fast_body(): lax.ppermute(pieces[turn], 'grp', [(at, at ^ turn) for at in range(groups)])  1.92 us
    pallas_call x1, Pallas kernels, fast_body(): pl.pallas_call(begin_kernel, out_shape=[jax.ShapeDtypeStruct((2,) + sourc...  1.63 us
  transfers between devices with their start and end apart: 9, of which 3 were waited for; matrix products, arithmetic and copies ran while one was open for 0% of the time, Pallas kernels for 3%

profile of v3, /device:TPU:0, one launch (start us, length us, event | category | flops | bytes accessed | tf_op | source)
XLA Modules:
  0.0 54.2 jit_solution(3927377827209220109)
XLA Ops:
  0.6 1.6 %begin.1 = (f32[2,4,8,512]{3,2,1,0:T(8,128)S(1)}, s32[4,8,512]{2,1,0:T(8,128)S(1)}, f32[256,256]{1,0:T(8,128)S(1)}, f32[8,3,128]{2,1,0:T(4,128)S(1)}) custom-call(f32[4,8,512]{2,1,0:T(8,128)} %bitcast.4, f32[4,8,512]{2,1,0:T(8,128)} %diagonal_from.1, s32[4,8,512]{2,1,0:T(8,128)} %ids_from.1, f32[256,256]{1,0:T(8,128)} %inverse_from.1), custom_call_target="tpu_custom_call" | custom-call | tf_op jit(solution)/shard_map/begin/pallas_call | solution.py:374
  2.3 3.1 %collective-permute-start.4 = (f32[2,4,8,512]{3,2,1,0:T(8,128)S(1)}, f32[2,4,8,512]{3,2,1,0:T(8,128)S(1)}, u32[]{:S(2)}, u32[]{:S(2)}) collective-permute-start(f32[2,4,8,512]{3,2,1,0:T(8,128)S(1)} %get-tuple-element.17.own_ref), channel_id=1, source_target_pairs={{0,4},{1,6},{2,5},{3,7},{4,0},{5,2},{6,1},{7,3},{8,12},{9,14},{10,... | collective-permute-start | bytes 393224 | tf_op jit(solution)/shard_map/ppermute | solution.py:390
  5.3 0.7 %collective-permute-start.3 = (f32[2,4,8,512]{3,2,1,0:T(8,128)S(1)}, f32[2,4,8,512]{3,2,1,0:T(8,128)S(1)}, u32[]{:S(2)}, u32[]{:S(2)}) collective-permute-start(f32[2,4,8,512]{3,2,1,0:T(8,128)S(1)} %get-tuple-element.17.own_ref), channel_id=1, source_target_pairs={{0,0},{1,2},{2,1},{3,3},{4,4},{5,6},{6,5},{7,7},{8,8},{9,10},{10,9... | collective-permute-start | bytes 393224 | tf_op jit(solution)/shard_map/ppermute | solution.py:390
  6.0 4.3 %collective-permute-start.2 = (f32[2,4,8,512]{3,2,1,0:T(8,128)S(1)}, f32[2,4,8,512]{3,2,1,0:T(8,128)S(1)}, u32[]{:S(2)}, u32[]{:S(2)}) collective-permute-start(f32[2,4,8,512]{3,2,1,0:T(8,128)S(1)} %get-tuple-element.17.own_ref), channel_id=1, source_target_pairs={{0,5},{1,4},{2,7},{3,6},{4,1},{5,0},{6,3},{7,2},{8,13},{9,12},{10,... | collective-permute-start | bytes 393224 | tf_op jit(solution)/shard_map/ppermute | solution.py:390
  10.3 0.1 collective-permute-start.1
  10.4 1.4 %collective-permute-start = (f32[2,4,8,512]{3,2,1,0:T(8,128)S(1)}, f32[2,4,8,512]{3,2,1,0:T(8,128)S(1)}, u32[]{:S(2)}, u32[]{:S(2)}) collective-permute-start(f32[2,4,8,512]{3,2,1,0:T(8,128)S(1)} %get-tuple-element.17.own_ref), channel_id=1, source_target_pairs={{0,4},{1,5},{2,6},{3,7},{4,0},{5,1},{6,2},{7,3},{8,12},{9,13},{10,... | collective-permute-start | bytes 393224 | tf_op jit(solution)/shard_map/ppermute | solution.py:390
  11.8 10.7 %all_to_all.15.gathered_ref = f32[8,3,128]{2,1,0:T(4,128)S(1)} all-to-all(f32[8,3,128]{2,1,0:T(4,128)S(1)} %get-tuple-element.20), channel_id=1, replica_groups=mesh['grp'=4,'gx'=2,'gy'=4] {'gx','gy'}, dimensions={0} | all-to-all | bytes 24576 | tf_op jit(solution)/shard_map/all_to_all | solution.py:345
  22.5 0.0 collective-permute-done.4.odd_other_ref
  22.5 0.0 collective-permute-done.3.odd_ref
  22.5 0.0 collective-permute-done.2.even_other_ref
  22.5 0.0 collective-permute-done.1.even_ref
  22.5 0.0 collective-permute-done.other_ref
  22.5 3.2 %shard_map.121 = (f32[10,24,512]{2,1,0:T(8,128)S(1)}, f32[8,24,512]{2,1,0:T(8,128)S(1)}, f32[8,24,512]{2,1,0:T(8,128)S(1)}, f32[8,3,128]{2,1,0:T(4,128)S(1)}) custom-call(f32[2,4,8,512]{3,2,1,0:T(8,128)S(1)} %get-tuple-element.17.own_ref, f32[2,4,8,512]{3,2,1,0:T(8,128)S(1)} %collective-permute-done.other_ref, ...), custom_call_target="tpu_custom_call" | custom-call | tf_op jit(solution)/shard_map/pallas_call | solution.py:329
  25.7 0.0 copy-start
  25.8 9.1 %all_to_all.16.gathered_ref = f32[8,3,128]{2,1,0:T(4,128)S(1)} all-to-all(f32[8,3,128]{2,1,0:T(4,128)S(1)} %get-tuple-element.24), channel_id=1, replica_groups=mesh['grp'=4,'gx'=2,'gy'=4] {'gx','gy'}, dimensions={0} | all-to-all | bytes 24576 | tf_op jit(solution)/shard_map/all_to_all | solution.py:345
  34.9 0.0 copy-start.1
  34.9 2.0 %shard_map.122 = (f32[4,8,128]{2,1,0:T(8,128)S(1)}, f32[4,8,128]{2,1,0:T(8,128)S(1)}, f32[4,8,128]{2,1,0:T(8,128)S(1)}, f32[4,8,128]{2,1,0:T(8,128)S(1)}) custom-call(f32[10,24,512]{2,1,0:T(8,128)S(1)} %get-tuple-element.21.field_ref, f32[8,24,512]{2,1,0:T(8,128)S(1)} %get-tuple-element.22.weight_ref, f32[8,24,512]{2,1,0:T(8,128)S(1)} %get-tuple-element.23.drive_ref, ...), custom_call_target="tpu_custom_call" | custom-call | tf_op jit(solution)/shard_map/pallas_call | solution.py:329
  36.9 0.1 collective-permute-start.5
  36.9 1.6 %collective-permute-start.6 = (f32[4,8,128]{2,1,0:T(8,128)S(1)}, f32[4,8,128]{2,1,0:T(8,128)S(1)}, u32[]{:S(2)}, u32[]{:S(2)}) collective-permute-start(f32[4,8,128]{2,1,0:T(8,128)S(1)} %get-tuple-element.27), channel_id=1, source_target_pairs={{0,16},{8,24},{16,0},{24,8},{1,17},{9,25},{17,1},{25,9},{2,18},{10... | collective-permute-start | bytes 49160 | tf_op jit(solution)/shard_map/ppermute | solution.py:408
  38.5 0.3 collective-permute-start.7
  38.8 0.0 collective-permute-done.5.rest_1_
  38.8 2.0 %collective-permute-done.6.rest_2_ = f32[4,8,128]{2,1,0:T(8,128)S(1)} collective-permute-done((f32[4,8,128]{2,1,0:T(8,128)S(1)}, f32[4,8,128]{2,1,0:T(8,128)S(1)}, u32[]{:S(2)}, u32[]{:S(2)}) %collective-permute-start.6) | collective-permute-done | bytes 16416 | tf_op jit(solution)/shard_map/ppermute | solution.py:408
  40.7 0.9 %collective-permute-done.7.rest_3_ = f32[4,8,128]{2,1,0:T(8,128)S(1)} collective-permute-done((f32[4,8,128]{2,1,0:T(8,128)S(1)}, f32[4,8,128]{2,1,0:T(8,128)S(1)}, u32[]{:S(2)}, u32[]{:S(2)}) %collective-permute-start.7) | collective-permute-done | bytes 16416 | tf_op jit(solution)/shard_map/ppermute | solution.py:408
  41.6 0.0 copy-done
  41.7 0.0 copy-done.1
  41.7 0.0 copy-start.2
  41.7 1.7 %shard_map.124 = f32[32,4,128]{2,1,0:T(4,128)} custom-call(f32[32,4,8,128]{3,2,1,0:T(8,128)S(1)} %copy-done.1, f32[64,4,8,128]{3,2,1,0:T(8,128)S(1)} %copy-done, f32[4,8,128]{2,1,0:T(8,128)S(1)} %get-tuple-element.25.rest_0_, f32[4,8,128]{2,1,0:T(8,128)S(1)} %collective-permute-done.5.rest_1_, f32[4,8,128]{2,1,0:T(8,128)S(1)} %collective-permute-done.6.rest_2_, ...), custom_call_target="tpu_custom_call" | custom-call | tf_op jit(solution)/shard_map/pallas_call | solution.py:329
  43.3 0.0 copy-start.4
  43.3 2.7 %all-to-all-start.2 = ((f32[32,4,128]{2,1,0:T(4,128)}), f32[32,4,128]{2,1,0:T(4,128)S(1)}, u32[]{:S(2)}, u32[]{:S(2)}) async-start(f32[32,4,128]{2,1,0:T(4,128)} %shard_map.124), calls=%async_computation.2 | async-start | bytes 131072 | tf_op jit(solution)/shard_map/all_to_all | solution.py:345
  46.0 0.0 copy-done.2
  46.0 0.0 copy-done.4
  46.0 0.0 copy-start.3
  46.1 0.0 copy-start.5
  46.1 1.5 %shard_map.123 = f32[32,4,8,128]{3,2,1,0:T(8,128)} custom-call(f32[4,32]{1,0:T(4,128)S(1)} %copy-done.4, f32[32,4,8,128]{3,2,1,0:T(8,128)S(1)} %copy-done.2, f32[4,8,128]{2,1,0:T(8,128)S(1)} %get-tuple-element.25.rest_0_, f32[4,8,128]{2,1,0:T(8,128)S(1)} %collective-permute-done.5.rest_1_, f32[4,8,128]{2,1,0:T(8,128)S(1)} %collective-permute-done.6.rest_2_, ...), custom_call_target="tpu_custom_call" | custom-call | tf_op jit(solution)/shard_map/pallas_call | solution.py:329
  47.6 5.7 %all-to-all-done.2.gathered_ref = f32[32,4,128]{2,1,0:T(4,128)S(1)} async-done(((f32[32,4,128]{2,1,0:T(4,128)}), f32[32,4,128]{2,1,0:T(4,128)S(1)}, u32[]{:S(2)}, u32[]{:S(2)}) %all-to-all-start.2) | async-done | bytes 65568 | tf_op jit(solution)/shard_map/all_to_all | solution.py:345
  53.3 0.0 copy-done.3
  53.3 0.0 copy-done.5
  53.3 0.9 %shard_map.125 = (f32[4,32]{1,0:T(4,128)}, f32[64,64]{1,0:T(8,128)}) custom-call(f32[32,4,128]{2,1,0:T(4,128)S(1)} %all-to-all-done.2.gathered_ref, f32[4,64]{1,0:T(4,128)S(1)} %bitcast.3, f32[64,64]{1,0:T(8,128)S(1)} %copy-done.3), custom_call_target="tpu_custom_call" | custom-call | tf_op jit(solution)/shard_map/pallas_call | solution.py:329
Async XLA Ops:
  2.3 20.2 %collective-permute-start.4 = (f32[2,4,8,512]{3,2,1,0:T(8,128)S(1)}, f32[2,4,8,512]{3,2,1,0:T(8,128)S(1)}, u32[]{:S(2)}, u32[]{:S(2)}) collective-permute-start(f32[2,4,8,512]{3,2,1,0:T(8,128)S(1)} %get-tuple-element.17.own_ref), channel_id=1, source_target_pairs={{0,4},{1,6},{2,5},{3,7},{4,0},{5,2},{6,1},{7,3},{8,12},{9,14},{10,... | collective-permute-start | bytes 393224 | tf_op jit(solution)/shard_map/ppermute | solution.py:390
  5.3 17.2 %collective-permute-start.3 = (f32[2,4,8,512]{3,2,1,0:T(8,128)S(1)}, f32[2,4,8,512]{3,2,1,0:T(8,128)S(1)}, u32[]{:S(2)}, u32[]{:S(2)}) collective-permute-start(f32[2,4,8,512]{3,2,1,0:T(8,128)S(1)} %get-tuple-element.17.own_ref), channel_id=1, source_target_pairs={{0,0},{1,2},{2,1},{3,3},{4,4},{5,6},{6,5},{7,7},{8,8},{9,10},{10,9... | collective-permute-start | bytes 393224 | tf_op jit(solution)/shard_map/ppermute | solution.py:390
  6.0 16.5 %collective-permute-start.2 = (f32[2,4,8,512]{3,2,1,0:T(8,128)S(1)}, f32[2,4,8,512]{3,2,1,0:T(8,128)S(1)}, u32[]{:S(2)}, u32[]{:S(2)}) collective-permute-start(f32[2,4,8,512]{3,2,1,0:T(8,128)S(1)} %get-tuple-element.17.own_ref), channel_id=1, source_target_pairs={{0,5},{1,4},{2,7},{3,6},{4,1},{5,0},{6,3},{7,2},{8,13},{9,12},{10,... | collective-permute-start | bytes 393224 | tf_op jit(solution)/shard_map/ppermute | solution.py:390
  10.3 12.2 %collective-permute-start.1 = (f32[2,4,8,512]{3,2,1,0:T(8,128)S(1)}, f32[2,4,8,512]{3,2,1,0:T(8,128)S(1)}, u32[]{:S(2)}, u32[]{:S(2)}) collective-permute-start(f32[2,4,8,512]{3,2,1,0:T(8,128)S(1)} %get-tuple-element.17.own_ref), channel_id=1, source_target_pairs={{0,1},{1,0},{2,3},{3,2},{4,5},{5,4},{6,7},{7,6},{8,9},{9,8},{10,11... | collective-permute-start | bytes 393224 | tf_op jit(solution)/shard_map/ppermute | solution.py:390
  10.4 12.1 %collective-permute-start = (f32[2,4,8,512]{3,2,1,0:T(8,128)S(1)}, f32[2,4,8,512]{3,2,1,0:T(8,128)S(1)}, u32[]{:S(2)}, u32[]{:S(2)}) collective-permute-start(f32[2,4,8,512]{3,2,1,0:T(8,128)S(1)} %get-tuple-element.17.own_ref), channel_id=1, source_target_pairs={{0,4},{1,5},{2,6},{3,7},{4,0},{5,1},{6,2},{7,3},{8,12},{9,13},{10,... | collective-permute-start | bytes 393224 | tf_op jit(solution)/shard_map/ppermute | solution.py:390
  25.7 15.9 %copy-start = (f32[64,4,8,128]{3,2,1,0:T(8,128)S(1)}, f32[64,4,8,128]{3,2,1,0:T(8,128)}, u32[]{:S(2)}) copy-start(f32[64,4,8,128]{3,2,1,0:T(8,128)} %phi_ref.1) | copy-start | bytes 3145732
  34.9 6.8 %copy-start.1 = (f32[32,4,8,128]{3,2,1,0:T(8,128)S(1)}, f32[32,4,8,128]{3,2,1,0:T(8,128)}, u32[]{:S(2)}) copy-start(f32[32,4,8,128]{3,2,1,0:T(8,128)} %psi_ref.1) | copy-start | bytes 1572868
  36.9 1.9 %collective-permute-start.5 = (f32[4,8,128]{2,1,0:T(8,128)S(1)}, f32[4,8,128]{2,1,0:T(8,128)S(1)}, u32[]{:S(2)}, u32[]{:S(2)}) collective-permute-start(f32[4,8,128]{2,1,0:T(8,128)S(1)} %get-tuple-element.26), channel_id=1, source_target_pairs={{0,8},{8,0},{16,24},{24,16},{1,9},{9,1},{17,25},{25,17},{2,10},{10... | collective-permute-start | bytes 49160 | tf_op jit(solution)/shard_map/ppermute | solution.py:408
  36.9 3.8 %collective-permute-start.6 = (f32[4,8,128]{2,1,0:T(8,128)S(1)}, f32[4,8,128]{2,1,0:T(8,128)S(1)}, u32[]{:S(2)}, u32[]{:S(2)}) collective-permute-start(f32[4,8,128]{2,1,0:T(8,128)S(1)} %get-tuple-element.27), channel_id=1, source_target_pairs={{0,16},{8,24},{16,0},{24,8},{1,17},{9,25},{17,1},{25,9},{2,18},{10... | collective-permute-start | bytes 49160 | tf_op jit(solution)/shard_map/ppermute | solution.py:408
  38.5 3.2 %collective-permute-start.7 = (f32[4,8,128]{2,1,0:T(8,128)S(1)}, f32[4,8,128]{2,1,0:T(8,128)S(1)}, u32[]{:S(2)}, u32[]{:S(2)}) collective-permute-start(f32[4,8,128]{2,1,0:T(8,128)S(1)} %get-tuple-element.28), channel_id=1, source_target_pairs={{0,24},{8,16},{16,8},{24,0},{1,25},{9,17},{17,9},{25,1},{2,26},{10... | collective-permute-start | bytes 49160 | tf_op jit(solution)/shard_map/ppermute | solution.py:408
  41.7 4.4 %copy-start.2 = (f32[32,4,8,128]{3,2,1,0:T(8,128)S(1)}, f32[32,4,8,128]{3,2,1,0:T(8,128)}, u32[]{:S(2)}) copy-start(f32[32,4,8,128]{3,2,1,0:T(8,128)} %range_ref.1) | copy-start | bytes 1572868
  43.3 2.7 %copy-start.4 = (f32[4,32]{1,0:T(4,128)S(1)}, f32[4,32]{1,0:T(4,128)}, u32[]{:S(2)}) copy-start(f32[4,32]{1,0:T(4,128)} %omega_ref.1) | copy-start | bytes 1540
  43.3 10.0 %all-to-all-start.2 = ((f32[32,4,128]{2,1,0:T(4,128)}), f32[32,4,128]{2,1,0:T(4,128)S(1)}, u32[]{:S(2)}, u32[]{:S(2)}) async-start(f32[32,4,128]{2,1,0:T(4,128)} %shard_map.124), calls=%async_computation.2 | async-start | bytes 131072 | tf_op jit(solution)/shard_map/all_to_all | solution.py:345
  46.0 7.3 %copy-start.3 = (f32[64,64]{1,0:T(8,128)S(1)}, f32[64,64]{1,0:T(8,128)}, u32[]{:S(2)}) copy-start(f32[64,64]{1,0:T(8,128)} %core_ref.1) | copy-start | bytes 49156
  46.1 7.2 %copy-start.5 = (f32[64,4]{0,1:T(4,128)S(1)}, f32[64,4]{0,1:T(4,128)}, u32[]{:S(2)}) copy-start(f32[64,4]{0,1:T(4,128)} %param.17) | copy-start | bytes 3076

commit v4 on v3

--- a/solution.py
+++ b/solution.py
@@ -103,7 +103,9 @@
     ranks_y = lax.bitwise_and(tile[0], XY_CUTS - 1)
     below_x = jnp.sum((ranks_x <= lanes[None]).astype(jnp.float32), axis=0)
     below_y = jnp.sum((ranks_y <= lanes - XY_CUTS).astype(jnp.float32), axis=0, keepdims=True)
-    store_copies(out_ref, lane_rows(row) + [jnp.where(lanes < XY_CUTS, below_x, below_y)])
+    rows = lane_rows(row) + [jnp.where(lanes < XY_CUTS, below_x, below_y)]
+    for at, part in enumerate(rows):
+        out_ref[at : at + 1, :] = part
     loads[2].wait()
     loads[3].wait()
 
@@ -206,7 +208,7 @@
             weight_ref[first_x + at, pl.ds(row, rows_y), :] = weight
             drive_ref[first_x + at, pl.ds(row, rows_y), :] = weight * ref[0, at]
 
-    gathered = jnp.sum(gathered_ref[...], axis=0)
+    gathered = gathered_ref[...]
     coarse = inverse_ref.shape[0]
     last = coarse // LANES
     cuts = cuts_of(gathered[last : last + 1], count_x, count_y)
@@ -377,7 +379,7 @@
             jax.ShapeDtypeStruct((2,) + source.shape, jnp.float32),
             jax.ShapeDtypeStruct(coarse_ids.shape, jnp.int32),
             jax.ShapeDtypeStruct(coarse_inverse.shape, jnp.float32),
-            jax.ShapeDtypeStruct(copies, jnp.float32),
+            jax.ShapeDtypeStruct(copies[1:], jnp.float32),
         ],
         in_specs=[pl.BlockSpec(memory_space=pltpu.HBM)] * 4,
         out_specs=[vmem] * 4,
@@ -385,11 +387,14 @@
         compiler_params=pltpu.CompilerParams(vmem_limit_bytes=VMEM_BYTES),
         name="begin",
     )(*map(in_hbm, (source, diagonal, coarse_ids, coarse_inverse)))
-    gathered = gather(begin, ("gx", "gy"))
-    others = [
-        lax.ppermute(mine, ("gx", "gy"), pairs(cross, phase))
-        for cross, phase in ((1, None), (0, 0), (1, 0), (0, 1), (1, 1))
-    ]
+    others = []
+    for at, (cross, phase) in enumerate(((1, None), (0, 0), (0, 0), (0, 1), (0, 1))):
+        sent = others[0] if at in (2, 4) else mine
+        others.append(lax.ppermute(sent, ("gx", "gy"), pairs(cross, phase)))
+    gathered = begin
+    turns = [("gx", count_x, 1)] + [("gy", count_y, 1 << bit) for bit in range(count_y.bit_length() - 1)]
+    for axis, count, bit in turns:
+        gathered = gathered + lax.ppermute(gathered, axis, [(i, i ^ bit) for i in range(count)])
     field, weight, drive, partial = call(
         functools.partial(first_kernel, counts, scale_factor),
         [padded, window, window, copies],
@@ -528,7 +533,8 @@
     coarse, groups = arrays[3].shape[0], lax.axis_size("grp")
     fits = (
         lax.axis_size("gx") == 2
-        and lax.axis_size("gy") % 2 == 0
+        and lax.axis_size("gy") & (lax.axis_size("gy") - 1) == 0
+        and lax.axis_size("gy") > 1
         and rows_y >= OUTER * SWEEPS
         and rows_y % SUBLANES == 0
         and groups & (groups - 1) == 0

time: 54.5 us -> 59.1 us (1.084)
  waiting for transfers between devices: 8.59 us -> 18.6 us
  blocking collectives: 19.8 us -> 10.1 us
  starting transfers between devices: 14.1 us -> 18.1 us
    ppermute x5 -> x8, waiting for transfers between devices: 0.01 us -> 10.1 us  [the longest x3 10.1 us: fast_body(): lax.ppermute(gathered, axis, [(i, i ^ bit) for i in range(count)])]
    all_to_all x2 -> x1, blocking collectives: 19.8 us -> 10.1 us  [gather(): return lax.all_to_all(copies, axes, 0, 0)]
    ppermute x5 -> x8, starting transfers between devices: 9.53 us -> 13.5 us  [the longest x5 11.9 us: fast_body(): others.append(lax.ppermute(sent, ('gx', 'gy'), pairs(cross, phase)))]
  transfers between devices with their start and end apart: 9 -> 12, of which waited for: 3 -> 6; matrix products, arithmetic and copies ran while one was open for 0% -> 0% of each run, Pallas kernels for 3% -> 3%
where the time goes in v4:
time: 59.1 us; the launch traced here: 58.9 us
  waiting for transfers between devices  18.6 us (31%)
  starting transfers between devices  18.1 us (31%)
  Pallas kernels  11.3 us (19%)
  blocking collectives  10.1 us (17%)
  between operations  0.76 us (1%)
    ppermute x5, starting transfers between devices, fast_body(): others.append(lax.ppermute(sent, ('gx', 'gy'), pairs(cross, phase)))  11.9 us
    all_to_all x1, blocking collectives, gather(): return lax.all_to_all(copies, axes, 0, 0)  10.1 us
    ppermute x3, waiting for transfers between devices, fast_body(): lax.ppermute(gathered, axis, [(i, i ^ bit) for i in range(count)])  10.1 us
    pallas_call x5, Pallas kernels, call(): pl.pallas_call(kernel, out_shape=shapes, in_specs=specs or [vmem] * len(i...  9.64 us
    all_to_all x1, waiting for transfers between devices, gather(): return lax.all_to_all(copies, axes, 0, 0)  5.7 us
    ppermute x3, waiting for transfers between devices, fast_body(): lax.ppermute(pieces[turn], 'grp', [(at, at ^ turn) for at in range(groups)])  2.87 us
    all_to_all x1, starting transfers between devices, gather(): return lax.all_to_all(copies, axes, 0, 0)  2.68 us
    ppermute x3, starting transfers between devices, fast_body(): lax.ppermute(pieces[turn], 'grp', [(at, at ^ turn) for at in range(groups)])  1.92 us
  transfers between devices with their start and end apart: 12, of which 6 were waited for; matrix products, arithmetic and copies ran while one was open for 0% of the time, Pallas kernels for 3%

profile of v4, /device:TPU:0, one launch (start us, length us, event | category | flops | bytes accessed | tf_op | source)
XLA Modules:
  0.0 58.9 jit_solution(11006604352702065390)
XLA Ops:
  0.6 1.6 %begin.1 = (f32[2,4,8,512]{3,2,1,0:T(8,128)S(1)}, s32[4,8,512]{2,1,0:T(8,128)S(1)}, f32[256,256]{1,0:T(8,128)S(1)}, f32[3,128]{1,0:T(4,128)S(1)}) custom-call(f32[4,8,512]{2,1,0:T(8,128)} %bitcast.4, f32[4,8,512]{2,1,0:T(8,128)} %diagonal_from.1, s32[4,8,512]{2,1,0:T(8,128)} %ids_from.1, f32[256,256]{1,0:T(8,128)} %inverse_from.1), custom_call_target="tpu_custom_call" | custom-call | tf_op jit(solution)/shard_map/begin/pallas_call | solution.py:376
  2.3 3.1 %collective-permute-start = (f32[2,4,8,512]{3,2,1,0:T(8,128)S(1)}, f32[2,4,8,512]{3,2,1,0:T(8,128)S(1)}, u32[]{:S(2)}, u32[]{:S(2)}) collective-permute-start(f32[2,4,8,512]{3,2,1,0:T(8,128)S(1)} %get-tuple-element.17.own_ref), channel_id=1, source_target_pairs={{0,4},{1,5},{2,6},{3,7},{4,0},{5,1},{6,2},{7,3},{8,12},{9,13},{10,... | collective-permute-start | bytes 393224 | tf_op jit(solution)/shard_map/ppermute | solution.py:393
  5.3 0.7 %collective-permute-start.3 = (f32[2,4,8,512]{3,2,1,0:T(8,128)S(1)}, f32[2,4,8,512]{3,2,1,0:T(8,128)S(1)}, u32[]{:S(2)}, u32[]{:S(2)}) collective-permute-start(f32[2,4,8,512]{3,2,1,0:T(8,128)S(1)} %get-tuple-element.17.own_ref), channel_id=1, source_target_pairs={{0,0},{1,2},{2,1},{3,3},{4,4},{5,6},{6,5},{7,7},{8,8},{9,10},{10,9... | collective-permute-start | bytes 393224 | tf_op jit(solution)/shard_map/ppermute | solution.py:393
  6.0 4.5 %collective-permute-start.1 = (f32[2,4,8,512]{3,2,1,0:T(8,128)S(1)}, f32[2,4,8,512]{3,2,1,0:T(8,128)S(1)}, u32[]{:S(2)}, u32[]{:S(2)}) collective-permute-start(f32[2,4,8,512]{3,2,1,0:T(8,128)S(1)} %get-tuple-element.17.own_ref), channel_id=1, source_target_pairs={{0,1},{1,0},{2,3},{3,2},{4,5},{5,4},{6,7},{7,6},{8,9},{9,8},{10,11... | collective-permute-start | bytes 393224 | tf_op jit(solution)/shard_map/ppermute | solution.py:393
  10.4 0.0 collective-permute-done.other_ref
  10.4 0.7 %collective-permute-start.4 = (f32[2,4,8,512]{3,2,1,0:T(8,128)S(1)}, f32[2,4,8,512]{3,2,1,0:T(8,128)S(1)}, u32[]{:S(2)}, u32[]{:S(2)}) collective-permute-start(f32[2,4,8,512]{3,2,1,0:T(8,128)S(1)} %collective-permute-done.other_ref), channel_id=1, source_target_pairs={{0,0},{1,2},{2,1},{3,3},{4,4},{5,6},{6,5},{7,7},{8,8},{9,10},{10,9... | collective-permute-start | bytes 393224 | tf_op jit(solution)/shard_map/ppermute | solution.py:393
  11.1 3.0 %collective-permute-start.2 = (f32[2,4,8,512]{3,2,1,0:T(8,128)S(1)}, f32[2,4,8,512]{3,2,1,0:T(8,128)S(1)}, u32[]{:S(2)}, u32[]{:S(2)}) collective-permute-start(f32[2,4,8,512]{3,2,1,0:T(8,128)S(1)} %collective-permute-done.other_ref), channel_id=1, source_target_pairs={{0,1},{1,0},{2,3},{3,2},{4,5},{5,4},{6,7},{7,6},{8,9},{9,8},{10,11... | collective-permute-start | bytes 393224 | tf_op jit(solution)/shard_map/ppermute | solution.py:393
  14.2 1.5 %collective-permute-start.5 = (f32[3,128]{1,0:T(4,128)S(1)}, f32[3,128]{1,0:T(4,128)S(1)}, u32[]{:S(2)}, u32[]{:S(2)}) collective-permute-start(f32[3,128]{1,0:T(4,128)S(1)} %get-tuple-element.20), channel_id=1, source_target_pairs={{0,4},{4,0},{1,5},{5,1},{2,6},{6,2},{3,7},{7,3},{8,12},{12,8},{9,1... | collective-permute-start | bytes 4616 | tf_op jit(solution)/shard_map/ppermute | solution.py:397
  15.7 2.1 %collective-permute-done.5 = f32[3,128]{1,0:T(4,128)S(1)} collective-permute-done((f32[3,128]{1,0:T(4,128)S(1)}, f32[3,128]{1,0:T(4,128)S(1)}, u32[]{:S(2)}, u32[]{:S(2)}) %collective-permute-start.5) | collective-permute-done | bytes 1568 | tf_op jit(solution)/shard_map/ppermute | solution.py:397
  17.8 0.1 collective-permute-start.6
  17.8 3.5 %collective-permute-done.6 = f32[3,128]{1,0:T(4,128)S(1)} collective-permute-done((f32[3,128]{1,0:T(4,128)S(1)}, f32[3,128]{1,0:T(4,128)S(1)}, u32[]{:S(2)}, u32[]{:S(2)}) %collective-permute-start.6) | collective-permute-done | bytes 1568 | tf_op jit(solution)/shard_map/ppermute | solution.py:397
  21.3 0.0 collective-permute-start.7
  21.3 4.5 %collective-permute-done.7 = f32[3,128]{1,0:T(4,128)S(1)} collective-permute-done((f32[3,128]{1,0:T(4,128)S(1)}, f32[3,128]{1,0:T(4,128)S(1)}, u32[]{:S(2)}, u32[]{:S(2)}) %collective-permute-start.7) | collective-permute-done | bytes 1568 | tf_op jit(solution)/shard_map/ppermute | solution.py:397
  25.8 0.0 collective-permute-done.3.odd_ref
  25.8 0.0 collective-permute-done.1.even_ref
  25.8 0.0 collective-permute-done.4.odd_other_ref
  25.9 0.0 collective-permute-done.2.even_other_ref
  25.9 3.4 %shard_map.121 = (f32[10,24,512]{2,1,0:T(8,128)S(1)}, f32[8,24,512]{2,1,0:T(8,128)S(1)}, f32[8,24,512]{2,1,0:T(8,128)S(1)}, f32[8,3,128]{2,1,0:T(4,128)S(1)}) custom-call(f32[2,4,8,512]{3,2,1,0:T(8,128)S(1)} %get-tuple-element.17.own_ref, f32[2,4,8,512]{3,2,1,0:T(8,128)S(1)} %collective-permute-done.other_ref, ...), custom_call_target="tpu_custom_call" | custom-call | tf_op jit(solution)/shard_map/pallas_call | solution.py:331
  29.3 0.0 copy-start
  29.3 10.1 %all_to_all.10.gathered_ref = f32[8,3,128]{2,1,0:T(4,128)S(1)} all-to-all(f32[8,3,128]{2,1,0:T(4,128)S(1)} %get-tuple-element.24), channel_id=1, replica_groups=mesh['grp'=4,'gx'=2,'gy'=4] {'gx','gy'}, dimensions={0} | all-to-all | bytes 24576 | tf_op jit(solution)/shard_map/all_to_all | solution.py:347
  39.4 0.0 copy-start.1
  39.4 2.1 %shard_map.122 = (f32[4,8,128]{2,1,0:T(8,128)S(1)}, f32[4,8,128]{2,1,0:T(8,128)S(1)}, f32[4,8,128]{2,1,0:T(8,128)S(1)}, f32[4,8,128]{2,1,0:T(8,128)S(1)}) custom-call(f32[10,24,512]{2,1,0:T(8,128)S(1)} %get-tuple-element.21.field_ref, f32[8,24,512]{2,1,0:T(8,128)S(1)} %get-tuple-element.22.weight_ref, f32[8,24,512]{2,1,0:T(8,128)S(1)} %get-tuple-element.23.drive_ref, ...), custom_call_target="tpu_custom_call" | custom-call | tf_op jit(solution)/shard_map/pallas_call | solution.py:331
  41.5 0.1 collective-permute-start.8
  41.6 1.6 %collective-permute-start.9 = (f32[4,8,128]{2,1,0:T(8,128)S(1)}, f32[4,8,128]{2,1,0:T(8,128)S(1)}, u32[]{:S(2)}, u32[]{:S(2)}) collective-permute-start(f32[4,8,128]{2,1,0:T(8,128)S(1)} %get-tuple-element.27), channel_id=1, source_target_pairs={{0,16},{8,24},{16,0},{24,8},{1,17},{9,25},{17,1},{25,9},{2,18},{10... | collective-permute-start | bytes 49160 | tf_op jit(solution)/shard_map/ppermute | solution.py:413
  43.1 0.3 collective-permute-start.10
  43.4 0.0 collective-permute-done.8.rest_1_
  43.4 2.0 %collective-permute-done.9.rest_2_ = f32[4,8,128]{2,1,0:T(8,128)S(1)} collective-permute-done((f32[4,8,128]{2,1,0:T(8,128)S(1)}, f32[4,8,128]{2,1,0:T(8,128)S(1)}, u32[]{:S(2)}, u32[]{:S(2)}) %collective-permute-start.9) | collective-permute-done | bytes 16416 | tf_op jit(solution)/shard_map/ppermute | solution.py:413
  45.4 0.9 %collective-permute-done.10.rest_3_ = f32[4,8,128]{2,1,0:T(8,128)S(1)} collective-permute-done((f32[4,8,128]{2,1,0:T(8,128)S(1)}, f32[4,8,128]{2,1,0:T(8,128)S(1)}, u32[]{:S(2)}, u32[]{:S(2)}) %collective-permute-start.10) | collective-permute-done | bytes 16416 | tf_op jit(solution)/shard_map/ppermute | solution.py:413
  46.3 0.0 copy-done
  46.3 0.0 copy-done.1
  46.3 0.0 copy-start.2
  46.3 1.7 %shard_map.124 = f32[32,4,128]{2,1,0:T(4,128)} custom-call(f32[32,4,8,128]{3,2,1,0:T(8,128)S(1)} %copy-done.1, f32[64,4,8,128]{3,2,1,0:T(8,128)S(1)} %copy-done, f32[4,8,128]{2,1,0:T(8,128)S(1)} %get-tuple-element.25.rest_0_, f32[4,8,128]{2,1,0:T(8,128)S(1)} %collective-permute-done.8.rest_1_, f32[4,8,128]{2,1,0:T(8,128)S(1)} %collective-permute-done.9.rest_2_, ...), custom_call_target="tpu_custom_call" | custom-call | tf_op jit(solution)/shard_map/pallas_call | solution.py:331
  48.0 0.0 copy-start.4
  48.0 2.7 %all-to-all-start.1 = ((f32[32,4,128]{2,1,0:T(4,128)}), f32[32,4,128]{2,1,0:T(4,128)S(1)}, u32[]{:S(2)}, u32[]{:S(2)}) async-start(f32[32,4,128]{2,1,0:T(4,128)} %shard_map.124), calls=%async_computation.1 | async-start | bytes 131072 | tf_op jit(solution)/shard_map/all_to_all | solution.py:347
  50.7 0.0 copy-done.2
  50.7 0.0 copy-done.4
  50.7 0.0 copy-start.3
  50.7 0.0 copy-start.5
  50.7 1.5 %shard_map.123 = f32[32,4,8,128]{3,2,1,0:T(8,128)} custom-call(f32[4,32]{1,0:T(4,128)S(1)} %copy-done.4, f32[32,4,8,128]{3,2,1,0:T(8,128)S(1)} %copy-done.2, f32[4,8,128]{2,1,0:T(8,128)S(1)} %get-tuple-element.25.rest_0_, f32[4,8,128]{2,1,0:T(8,128)S(1)} %collective-permute-done.8.rest_1_, f32[4,8,128]{2,1,0:T(8,128)S(1)} %collective-permute-done.9.rest_2_, ...), custom_call_target="tpu_custom_call" | custom-call | tf_op jit(solution)/shard_map/pallas_call | solution.py:331
  52.2 5.7 %all-to-all-done.1.gathered_ref = f32[32,4,128]{2,1,0:T(4,128)S(1)} async-done(((f32[32,4,128]{2,1,0:T(4,128)}), f32[32,4,128]{2,1,0:T(4,128)S(1)}, u32[]{:S(2)}, u32[]{:S(2)}) %all-to-all-start.1) | async-done | bytes 65568 | tf_op jit(solution)/shard_map/all_to_all | solution.py:347
  57.9 0.0 copy-done.3
  57.9 0.0 copy-done.5
  57.9 0.9 %shard_map.125 = (f32[4,32]{1,0:T(4,128)}, f32[64,64]{1,0:T(8,128)}) custom-call(f32[32,4,128]{2,1,0:T(4,128)S(1)} %all-to-all-done.1.gathered_ref, f32[4,64]{1,0:T(4,128)S(1)} %bitcast.3, f32[64,64]{1,0:T(8,128)S(1)} %copy-done.3), custom_call_target="tpu_custom_call" | custom-call | tf_op jit(solution)/shard_map/pallas_call | solution.py:331
  (3 shorter events, 0.0 us)
Async XLA Ops:
  2.3 8.2 %collective-permute-start = (f32[2,4,8,512]{3,2,1,0:T(8,128)S(1)}, f32[2,4,8,512]{3,2,1,0:T(8,128)S(1)}, u32[]{:S(2)}, u32[]{:S(2)}) collective-permute-start(f32[2,4,8,512]{3,2,1,0:T(8,128)S(1)} %get-tuple-element.17.own_ref), channel_id=1, source_target_pairs={{0,4},{1,5},{2,6},{3,7},{4,0},{5,1},{6,2},{7,3},{8,12},{9,13},{10,... | collective-permute-start | bytes 393224 | tf_op jit(solution)/shard_map/ppermute | solution.py:393
  5.3 20.5 %collective-permute-start.3 = (f32[2,4,8,512]{3,2,1,0:T(8,128)S(1)}, f32[2,4,8,512]{3,2,1,0:T(8,128)S(1)}, u32[]{:S(2)}, u32[]{:S(2)}) collective-permute-start(f32[2,4,8,512]{3,2,1,0:T(8,128)S(1)} %get-tuple-element.17.own_ref), channel_id=1, source_target_pairs={{0,0},{1,2},{2,1},{3,3},{4,4},{5,6},{6,5},{7,7},{8,8},{9,10},{10,9... | collective-permute-start | bytes 393224 | tf_op jit(solution)/shard_map/ppermute | solution.py:393
  6.0 19.8 %collective-permute-start.1 = (f32[2,4,8,512]{3,2,1,0:T(8,128)S(1)}, f32[2,4,8,512]{3,2,1,0:T(8,128)S(1)}, u32[]{:S(2)}, u32[]{:S(2)}) collective-permute-start(f32[2,4,8,512]{3,2,1,0:T(8,128)S(1)} %get-tuple-element.17.own_ref), channel_id=1, source_target_pairs={{0,1},{1,0},{2,3},{3,2},{4,5},{5,4},{6,7},{7,6},{8,9},{9,8},{10,11... | collective-permute-start | bytes 393224 | tf_op jit(solution)/shard_map/ppermute | solution.py:393
  10.4 15.4 %collective-permute-start.4 = (f32[2,4,8,512]{3,2,1,0:T(8,128)S(1)}, f32[2,4,8,512]{3,2,1,0:T(8,128)S(1)}, u32[]{:S(2)}, u32[]{:S(2)}) collective-permute-start(f32[2,4,8,512]{3,2,1,0:T(8,128)S(1)} %collective-permute-done.other_ref), channel_id=1, source_target_pairs={{0,0},{1,2},{2,1},{3,3},{4,4},{5,6},{6,5},{7,7},{8,8},{9,10},{10,9... | collective-permute-start | bytes 393224 | tf_op jit(solution)/shard_map/ppermute | solution.py:393
  11.1 14.7 %collective-permute-start.2 = (f32[2,4,8,512]{3,2,1,0:T(8,128)S(1)}, f32[2,4,8,512]{3,2,1,0:T(8,128)S(1)}, u32[]{:S(2)}, u32[]{:S(2)}) collective-permute-start(f32[2,4,8,512]{3,2,1,0:T(8,128)S(1)} %collective-permute-done.other_ref), channel_id=1, source_target_pairs={{0,1},{1,0},{2,3},{3,2},{4,5},{5,4},{6,7},{7,6},{8,9},{9,8},{10,11... | collective-permute-start | bytes 393224 | tf_op jit(solution)/shard_map/ppermute | solution.py:393
  14.2 3.6 %collective-permute-start.5 = (f32[3,128]{1,0:T(4,128)S(1)}, f32[3,128]{1,0:T(4,128)S(1)}, u32[]{:S(2)}, u32[]{:S(2)}) collective-permute-start(f32[3,128]{1,0:T(4,128)S(1)} %get-tuple-element.20), channel_id=1, source_target_pairs={{0,4},{4,0},{1,5},{5,1},{2,6},{6,2},{3,7},{7,3},{8,12},{12,8},{9,1... | collective-permute-start | bytes 4616 | tf_op jit(solution)/shard_map/ppermute | solution.py:397
  17.8 3.6 %collective-permute-start.6 = (f32[3,128]{1,0:T(4,128)S(1)}, f32[3,128]{1,0:T(4,128)S(1)}, u32[]{:S(2)}, u32[]{:S(2)}) collective-permute-start(f32[3,128]{1,0:T(4,128)S(1)} %add.9), channel_id=1, source_target_pairs={{0,1},{1,0},{2,3},{3,2},{4,5},{5,4},{6,7},{7,6},{8,9},{9,8},{10,11... | collective-permute-start | bytes 4616 | tf_op jit(solution)/shard_map/ppermute | solution.py:397
  21.3 4.5 %collective-permute-start.7 = (f32[3,128]{1,0:T(4,128)S(1)}, f32[3,128]{1,0:T(4,128)S(1)}, u32[]{:S(2)}, u32[]{:S(2)}) collective-permute-start(f32[3,128]{1,0:T(4,128)S(1)} %add.10), channel_id=1, source_target_pairs={{0,2},{1,3},{2,0},{3,1},{4,6},{5,7},{6,4},{7,5},{8,10},{9,11},{10,... | collective-permute-start | bytes 4616 | tf_op jit(solution)/shard_map/ppermute | solution.py:397
  29.3 17.1 %copy-start = (f32[64,4,8,128]{3,2,1,0:T(8,128)S(1)}, f32[64,4,8,128]{3,2,1,0:T(8,128)}, u32[]{:S(2)}) copy-start(f32[64,4,8,128]{3,2,1,0:T(8,128)} %phi_ref.1) | copy-start | bytes 3145732
  39.4 6.9 %copy-start.1 = (f32[32,4,8,128]{3,2,1,0:T(8,128)S(1)}, f32[32,4,8,128]{3,2,1,0:T(8,128)}, u32[]{:S(2)}) copy-start(f32[32,4,8,128]{3,2,1,0:T(8,128)} %psi_ref.1) | copy-start | bytes 1572868
  41.5 1.9 %collective-permute-start.8 = (f32[4,8,128]{2,1,0:T(8,128)S(1)}, f32[4,8,128]{2,1,0:T(8,128)S(1)}, u32[]{:S(2)}, u32[]{:S(2)}) collective-permute-start(f32[4,8,128]{2,1,0:T(8,128)S(1)} %get-tuple-element.26), channel_id=1, source_target_pairs={{0,8},{8,0},{16,24},{24,16},{1,9},{9,1},{17,25},{25,17},{2,10},{10... | collective-permute-start | bytes 49160 | tf_op jit(solution)/shard_map/ppermute | solution.py:413
  41.6 3.8 %collective-permute-start.9 = (f32[4,8,128]{2,1,0:T(8,128)S(1)}, f32[4,8,128]{2,1,0:T(8,128)S(1)}, u32[]{:S(2)}, u32[]{:S(2)}) collective-permute-start(f32[4,8,128]{2,1,0:T(8,128)S(1)} %get-tuple-element.27), channel_id=1, source_target_pairs={{0,16},{8,24},{16,0},{24,8},{1,17},{9,25},{17,1},{25,9},{2,18},{10... | collective-permute-start | bytes 49160 | tf_op jit(solution)/shard_map/ppermute | solution.py:413
  43.1 3.2 %collective-permute-start.10 = (f32[4,8,128]{2,1,0:T(8,128)S(1)}, f32[4,8,128]{2,1,0:T(8,128)S(1)}, u32[]{:S(2)}, u32[]{:S(2)}) collective-permute-start(f32[4,8,128]{2,1,0:T(8,128)S(1)} %get-tuple-element.28), channel_id=1, source_target_pairs={{0,24},{8,16},{16,8},{24,0},{1,25},{9,17},{17,9},{25,1},{2,26},{10... | collective-permute-start | bytes 49160 | tf_op jit(solution)/shard_map/ppermute | solution.py:413
  46.3 4.4 %copy-start.2 = (f32[32,4,8,128]{3,2,1,0:T(8,128)S(1)}, f32[32,4,8,128]{3,2,1,0:T(8,128)}, u32[]{:S(2)}) copy-start(f32[32,4,8,128]{3,2,1,0:T(8,128)} %range_ref.1) | copy-start | bytes 1572868
  48.0 2.7 %copy-start.4 = (f32[4,32]{1,0:T(4,128)S(1)}, f32[4,32]{1,0:T(4,128)}, u32[]{:S(2)}) copy-start(f32[4,32]{1,0:T(4,128)} %omega_ref.1) | copy-start | bytes 1540
  48.0 10.0 %all-to-all-start.1 = ((f32[32,4,128]{2,1,0:T(4,128)}), f32[32,4,128]{2,1,0:T(4,128)S(1)}, u32[]{:S(2)}, u32[]{:S(2)}) async-start(f32[32,4,128]{2,1,0:T(4,128)} %shard_map.124), calls=%async_computation.1 | async-start | bytes 131072 | tf_op jit(solution)/shard_map/all_to_all | solution.py:347
  50.7 7.3 %copy-start.3 = (f32[64,64]{1,0:T(8,128)S(1)}, f32[64,64]{1,0:T(8,128)}, u32[]{:S(2)}) copy-start(f32[64,64]{1,0:T(8,128)} %core_ref.1) | copy-start | bytes 49156
  50.7 7.2 %copy-start.5 = (f32[64,4]{0,1:T(4,128)S(1)}, f32[64,4]{0,1:T(4,128)}, u32[]{:S(2)}) copy-start(f32[64,4]{0,1:T(4,128)} %param.17) | copy-start | bytes 3076
